TPU v7x, 512 devices: a whole 4x4x16 slice. The times are simulated.
512 devices in a mesh: az: 32 (over z, y_lo), rad: 8 (over x, core), tool: 2 (over y_hi).
Axes of the slice: x: 4, y: 4 (y_hi: 2, y_lo: 2; y = y_hi * 2 + y_lo), z: 16, core: 2. Of those that a mesh axis runs over, the one named last changes fastest.
Arguments:
- dwell: float32 [4, 256, 32768], P('tool', 'rad', 'az'), may hold values from -6 to 6
- residual: float32 [256, 32768], P('rad', 'az')
- influence: bfloat16 [4, 64, 64], P('tool')
- cycle_start: int32 [256], P('rad'), may hold values from 0 to 8191
- cycle_end: int32 [256], P('rad'), may hold values from 24577 to 32768
- allowed_bits: int32 [4, 256, 2048], P('tool', 'rad', 'az'), may hold values from 0 to 65535
Outputs:
- dwell_new: float32 [4, 256, 32768], P('tool', 'rad', 'az')
- residual_new: float32 [256, 32768], P('rad', ('az', 'tool'))
- direction_new: float32 [4, 256, 32768], P('tool', 'rad', 'az')
All inputs are finite; a program needn't handle non-finite values.
Results may differ from a plain program's by a relative error of at most 0.0003.
Values may be sent and summed in bfloat16 or wider, within the bound.
A program may use at most 64 MiB of HBM per device.

v0:
```python
import functools

import jax
import jax.numpy as jnp
from jax import lax
from jax.sharding import Mesh
from jax.sharding import PartitionSpec as P

AZ = ("az_0", "az_1")
RAD = ("rad_0", "rad_1")
AZ_RAD_TOOL = ("az_0", "az_1", "rad_0", "rad_1", "tool")
AZ_RAD = ("az_0", "az_1", "rad_0", "rad_1")
AZ_TOOL = ("az_0", "az_1", "tool")


EPSILON = 1e-06
GROUP_ROWS = 8


def padded_2(array, sides, width, wrap):
    for axis, dim in sides:
        devices, length = (lax.axis_size(axis), array.shape[dim])
        up = [(i, (i + 1) % devices) for i in range(devices if wrap else devices - 1)]
        down = [(j, i) for i, j in up]
        last = lax.slice_in_dim(array, length - width, length, axis=dim)
        leading = lax.slice_in_dim(array, 0, width, axis=dim)
        before = lax.ppermute(last, axis, up)
        after = lax.ppermute(leading, axis, down)
        array = jnp.concatenate([before, array, after], axis=dim)
    return array


def one_axis_at_a_time(array, axes):
    return functools.reduce(lax.psum, axes, array)


def copy_for_each(array, axis):
    devices = lax.axis_size(axis)
    return lax.all_to_all(
        jnp.broadcast_to(array[None], (devices, *array.shape)), axis, 0, 0, tiled=True
    )


def of_everyone(array, axis):
    return copy_for_each(array, axis).sum(axis=0)


def band_table(kernel, block_width):
    extent = kernel.shape[-1]
    span = block_width + extent
    inputs = jnp.arange(span, dtype=jnp.int32)[None, :, None]
    outputs = jnp.arange(block_width, dtype=jnp.int32)[None, None, :]
    offsets = jnp.arange(extent, dtype=jnp.int32)[:, None, None]
    selector = (inputs - outputs == offsets).astype(jnp.bfloat16)
    return jnp.einsum("tij,jpw->tipw", kernel, selector, preferred_element_type=jnp.float32).astype(
        jnp.bfloat16
    )


def correlate(padded, band, pattern, acc_shape, block_width):
    lead_count, padded_rows, padded_cols = padded.shape
    extent = band.shape[1]
    row_count = padded_rows - extent
    sector_width = padded_cols - extent
    block_count = sector_width // block_width
    padded = jnp.pad(padded, ((0, 0), (0, 0), (0, block_width - extent)))
    leading = padded[:, :, :sector_width].reshape(lead_count, padded_rows, block_count, block_width)
    trailing = padded[:, :, block_width : block_width + sector_width].reshape(
        lead_count, padded_rows, block_count, block_width
    )
    windows = jnp.concatenate([leading, trailing[:, :, :, :extent]], axis=3)

    def group_turn(group_index, running):
        first_row = group_index * GROUP_ROWS
        stacked = jnp.stack(
            [
                lax.dynamic_slice_in_dim(windows, first_row + offset, row_count, 1)
                for offset in range(GROUP_ROWS)
            ],
            axis=1,
        )
        band_rows = lax.dynamic_slice_in_dim(band, first_row, GROUP_ROWS, 1)
        return running + jnp.einsum(pattern, stacked, band_rows, preferred_element_type=jnp.float32)

    running = lax.fori_loop(0, extent // GROUP_ROWS, group_turn, jnp.zeros(acc_shape, jnp.float32))
    return running.reshape(running.shape[:-2] + (sector_width,))


def extend(values, halo_reach):
    widened = padded_2(values, ((AZ, 2),), halo_reach, True)
    return padded_2(widened, ((RAD, 1),), halo_reach, False)


def per_device(dwell, residual, influence, cycle_start, cycle_end, allowed_bits):
    tool_count, cycle_count, sector_width = dwell.shape
    extent = influence.shape[-1]
    halo_reach = extent // 2
    block_width = 128
    block_count = sector_width // block_width
    columns = lax.axis_index(AZ) * sector_width + jnp.arange(sector_width, dtype=jnp.int32)
    inside = (
        (columns[None, :] >= cycle_start[:, None]) & (columns[None, :] < cycle_end[:, None])
    ).astype(jnp.float32)
    bit_shift = jnp.arange(sector_width, dtype=jnp.int32) % 16
    allowed = (jnp.repeat(allowed_bits, 16, axis=2) >> bit_shift & 1).astype(jnp.float32)
    forward_band = band_table(influence, block_width)
    adjoint_band = band_table(influence[:, ::-1, ::-1], block_width)

    def adjoint(field_low):
        padded = extend(field_low[None], halo_reach)
        shifted = jnp.pad(padded[:, 1:, 1:], ((0, 0), (0, 1), (0, 1)))
        spread = correlate(
            shifted,
            adjoint_band,
            "lkrbp,tkpw->trbw",
            (tool_count, cycle_count, block_count, block_width),
            block_width,
        )
        return allowed * spread

    first_low = (inside * residual).astype(jnp.bfloat16)
    gradient = adjoint(first_low)
    local_first = jnp.sum(gradient * gradient)
    gamma = one_axis_at_a_time(local_first, AZ_RAD_TOOL)
    direction_low = gradient.astype(jnp.bfloat16)
    removal = inside * correlate(
        extend(direction_low, halo_reach),
        forward_band,
        "tkrbp,tkpw->rbw",
        (cycle_count, block_count, block_width),
        block_width,
    )
    share_width = sector_width // lax.axis_size("tool")
    share_start = lax.axis_index("tool") * share_width
    removal_full = of_everyone(removal, "tool")
    curvature = one_axis_at_a_time(jnp.sum(removal_full * removal_full), AZ_RAD)
    step_size = gamma / (curvature + EPSILON)
    residual_full = residual - step_size * removal_full
    second_low = (inside * residual_full).astype(jnp.bfloat16)
    residual_new = lax.dynamic_slice_in_dim(residual_full, share_start, share_width, 1)
    dwell_new = dwell + step_size * gradient
    gradient_new = adjoint(second_low)
    gamma_new = one_axis_at_a_time(jnp.sum(gradient_new * gradient_new), AZ_RAD_TOOL)
    direction_new = gradient_new + gamma_new / (gamma + EPSILON) * gradient
    return (dwell_new, residual_new, direction_new)


def solution(mesh):
    torus = Mesh(
        mesh.devices.reshape(16, 2, 4, 2, mesh.shape["tool"]),
        ("az_0", "az_1", "rad_0", "rad_1", "tool"),
    )
    in_specs = (
        P("tool", RAD, AZ),
        P(RAD, AZ),
        P("tool", None, None),
        P(RAD),
        P(RAD),
        P("tool", RAD, AZ),
    )
    out_specs = (P("tool", RAD, AZ), P(RAD, AZ_TOOL), P("tool", RAD, AZ))
    return jax.shard_map(
        per_device, mesh=torus, in_specs=in_specs, out_specs=out_specs, check_vma=False
    )
```

profile of v0, /device:TPU:1, one launch (start us, length us, event | category | flops | bytes accessed | tf_op | source)
XLA Modules:
  0.0 447.5 jit_solution(5594094641950925820)
XLA Ops:
  1.7 4.0 collective-permute-start
  5.8 10.9 %collective-permute-start.1 = (bf16[1,32,32]{2,1,0:T(8,128)(2,1)S(1)}, bf16[1,32,32]{2,1,0:T(8,128)(2,1)S(1)}, u32[]{:S(2)}, u32[]{:S(2)}) collective-permute-start(bf16[1,32,32]{2,1,0:T(8,128)(2,1)S(1)} %get-tuple-element.517), channel_id=1, source_target_pairs={{16,0},{32,16},{48,32},{64,48},{80,64},{96,80},{112,96},{128,112},... | collective-permute-start | bytes 6152 | tf_op jit(solution)/shard_map/ppermute | solution.py:28
  17.5 4.5 convert_bitcast_fusion.1
  22.0 9.5 %copy.81 = bf16[2,64,192,128]{3,2,1,0:T(8,128)(2,1)} copy(bf16[2,64,192,128]{3,1,0,2:T(8,128)(2,1)} %convert_bitcast_fusion.1) | data formatting | bytes 12582912
  31.7 4.0 collective-permute-start.2
  35.7 1.9 collective-permute-start.3
  37.6 3.7 collective-permute-done.3
  42.5 75.2 %while.48 = (s32[]{:T(128)}, f32[2,32,8,128]{3,1,2,0:T(8,128)S(1)}, bf16[2,64,192,128]{3,2,1,0:T(8,128)(2,1)}, bf16[1,96,8,192]{3,1,2,0:T(8,128)(2,1)}, s32[]{:T...) while((s32[]{:T(128)}, f32[2,32,8,128]{3,1,2,0:T(8,128)S(1)}, ...), condition=%wide.region_1.2_spmd.clone, body=%wide.region_0.1_spmd.clone.sunk | while | flops 201457696 | bytes 3932796 | solution.py:85
  50.3 1.6 fusion.74
  69.1 1.6 fusion.74
  78.5 1.6 fusion.74
  87.9 1.6 fusion.74
  97.3 1.6 fusion.74
  106.8 1.6 fusion.74
  116.2 1.6 fusion.74
  119.1 1.9 collective-permute-start.4
  121.0 5.5 %collective-permute-start.5 = (bf16[2,32,32]{1,2,0:T(8,128)(2,1)S(1)}, bf16[2,32,32]{1,2,0:T(8,128)(2,1)S(1)}, u32[]{:S(2)}, u32[]{:S(2)}) collective-permute-start(bf16[2,32,32]{1,2,0:T(8,128)(2,1)S(1)} %get-tuple-element.507), channel_id=1, source_target_pairs={{16,0},{32,16},{48,32},{64,48},{80,64},{96,80},{112,96},{128,112},... | collective-permute-start | bytes 12296 | tf_op jit(solution)/shard_map/ppermute | solution.py:28
  127.6 3.0 collective-permute-start.6
  130.6 2.1 collective-permute-start.7
  132.8 4.5 convert_bitcast_fusion
  139.1 79.6 %while.49 = (s32[]{:T(128)}, f32[32,8,128]{2,1,0:T(8,128)S(1)}, bf16[2,96,8,192]{3,2,0,1:T(8,128)(2,1)}, bf16[2,64,192,128]{3,1,0,2:T(8,128)(2,1)}, s32[]{:T(128...) while((s32[]{:T(128)}, f32[32,8,128]{2,1,0:T(8,128)S(1)}, ...), condition=%wide.region_9.10_spmd.clone, body=%wide.region_8.9_spmd.clone.sunk | while | flops 201392160 | bytes 7864956 | solution.py:85
  219.5 3.9 all-to-all-start
  223.4 1.7 fusion.36
  225.1 4.8 %all-to-all-done = f32[2,32,1024]{2,1,0:T(8,128)S(1)} async-done(((f32[2,32,1024]{2,1,0:T(8,128)}), f32[2,32,1024]{2,1,0:T(8,128)S(1)}, u32[]{:S(2)}, u32[]{:S(2)}) %all-to-all-start) | async-done | bytes 262176 | tf_op jit(solution)/shard_map/all_to_all | solution.py:39
  230.5 21.6 %all-reduce.5 = (f32[]{:T(128)}, f32[]{:T(128)}) all-reduce(f32[]{:T(128)} %fusion.36, f32[]{:T(128)} %multiply_reduce_fusion), channel_id=1, replica_groups=mesh['az_0'=16,'az_1'=2,'rad_0'=4,'rad_1'=2,'tool'=2] {'az_0'}, use_global_device_ids=true, to_apply=%region_3.4 | all-reduce | flops 2 | bytes 16 | tf_op jit(solution)/shard_map/psum | solution.py:34
  252.1 6.3 %all-reduce.8 = (f32[]{:T(128)}, f32[]{:T(128)}) all-reduce(f32[]{:T(128)} %get-tuple-element.495, f32[]{:T(128)} %get-tuple-element.496), channel_id=1, replica_groups=mesh['az_0'=16,'az_1'=2,'rad_0'=4,'rad_1'=2,'tool'=2] {'az_1'}, use_global_device_ids=true, to_apply=%region_4.5 | all-reduce | flops 2 | bytes 16 | tf_op jit(solution)/shard_map/psum | solution.py:34
  258.4 7.3 %all-reduce.6 = (f32[]{:T(128)}, f32[]{:T(128)}) all-reduce(f32[]{:T(128)} %get-tuple-element.501, f32[]{:T(128)} %get-tuple-element.502), channel_id=1, replica_groups=mesh['az_0'=16,'az_1'=2,'rad_0'=4,'rad_1'=2,'tool'=2] {'rad_0'}, use_global_device_ids=true, to_apply=%region_5.6 | all-reduce | flops 2 | bytes 16 | tf_op jit(solution)/shard_map/psum | solution.py:34
  265.8 15.2 %all-reduce.7 = (f32[]{:T(128)}, f32[]{:T(128)}) all-reduce(f32[]{:T(128)} %get-tuple-element.497, f32[]{:T(128)} %get-tuple-element.498), channel_id=1, replica_groups=mesh['az_0'=16,'az_1'=2,'rad_0'=4,'rad_1'=2,'tool'=2] {'rad_1'}, use_global_device_ids=true, to_apply=%region_6.7 | all-reduce | flops 2 | bytes 16 | tf_op jit(solution)/shard_map/psum | solution.py:34
  281.0 5.9 %psum.102 = f32[]{:T(128)} all-reduce(f32[]{:T(128)} %get-tuple-element.499), channel_id=1, replica_groups=mesh['az_0'=16,'az_1'=2,'rad_0'=4,'rad_1'=2,'tool'=2] {'tool'}, use_global_device_ids=true, to_apply=%region_7.8 | all-reduce | flops 1 | bytes 8 | tf_op jit(solution)/shard_map/psum | solution.py:34
  288.4 3.7 collective-permute-start.8
  292.0 3.7 collective-permute-start.9
  296.9 3.8 collective-permute-start.10
  300.7 2.0 collective-permute-start.11
  302.7 3.6 collective-permute-done.11
  307.5 75.3 %while.50 = (s32[]{:T(128)}, f32[2,32,8,128]{3,1,2,0:T(8,128)S(1)}, bf16[2,64,192,128]{3,2,1,0:T(8,128)(2,1)}, bf16[1,96,8,192]{3,1,2,0:T(8,128)(2,1)}, s32[]{:T...) while((s32[]{:T(128)}, f32[2,32,8,128]{3,1,2,0:T(8,128)S(1)}, ...), condition=%wide.region_17.18_spmd.clone, body=%wide.region_16.17_spmd.clone.sunk | while | flops 201457696 | bytes 3932796 | solution.py:85
  315.3 1.6 fusion.79
  324.8 1.6 fusion.79
  353.0 1.6 fusion.79
  362.4 1.6 fusion.79
  371.8 1.6 fusion.79
  384.6 21.2 %psum.107 = f32[]{:T(128)} all-reduce(f32[]{:T(128)} %fusion.34), channel_id=1, replica_groups=mesh['az_0'=16,'az_1'=2,'rad_0'=4,'rad_1'=2,'tool'=2] {'az_0'}, use_global_device_ids=true, to_apply=%region_19.20 | all-reduce | flops 1 | bytes 8 | tf_op jit(solution)/shard_map/psum | solution.py:34
  405.8 6.8 %psum.108 = f32[]{:T(128)} all-reduce(f32[]{:T(128)} %psum.107), channel_id=1, replica_groups=mesh['az_0'=16,'az_1'=2,'rad_0'=4,'rad_1'=2,'tool'=2] {'az_1'}, use_global_device_ids=true, to_apply=%region_20.21 | all-reduce | flops 1 | bytes 8 | tf_op jit(solution)/shard_map/psum | solution.py:34
  413.3 7.7 %psum.109 = f32[]{:T(128)} all-reduce(f32[]{:T(128)} %psum.108), channel_id=1, replica_groups=mesh['az_0'=16,'az_1'=2,'rad_0'=4,'rad_1'=2,'tool'=2] {'rad_0'}, use_global_device_ids=true, to_apply=%region_21.22 | all-reduce | flops 1 | bytes 8 | tf_op jit(solution)/shard_map/psum | solution.py:34
  421.6 11.8 %psum.110 = f32[]{:T(128)} all-reduce(f32[]{:T(128)} %psum.109), channel_id=1, replica_groups=mesh['az_0'=16,'az_1'=2,'rad_0'=4,'rad_1'=2,'tool'=2] {'rad_1'}, use_global_device_ids=true, to_apply=%region_22.23 | all-reduce | flops 1 | bytes 8 | tf_op jit(solution)/shard_map/psum | solution.py:34
  434.7 5.9 %psum.111 = f32[]{:T(128)} all-reduce(f32[]{:T(128)} %psum.110), channel_id=1, replica_groups=mesh['az_0'=16,'az_1'=2,'rad_0'=4,'rad_1'=2,'tool'=2] {'tool'}, use_global_device_ids=true, to_apply=%region_23.24 | all-reduce | flops 1 | bytes 8 | tf_op jit(solution)/shard_map/psum | solution.py:34
  441.3 1.7 fusion.22
  443.0 2.2 copy.96
  445.3 2.2 copy.97
  (292 shorter events, 222.9 us)
Async XLA Ops:
  1.7 29.8 %collective-permute-start = (bf16[1,32,32]{2,1,0:T(8,128)(2,1)S(1)}, bf16[1,32,32]{2,1,0:T(8,128)(2,1)S(1)}, u32[]{:S(2)}, u32[]{:S(2)}) collective-permute-start(bf16[1,32,32]{2,1,0:T(8,128)(2,1)S(1)} %get-tuple-element.518), channel_id=1, source_target_pairs={{0,16},{16,32},{32,48},{48,64},{64,80},{80,96},{96,112},{112,128},... | collective-permute-start | bytes 6152 | tf_op jit(solution)/shard_map/ppermute | solution.py:27
  5.8 25.8 %collective-permute-start.1 = (bf16[1,32,32]{2,1,0:T(8,128)(2,1)S(1)}, bf16[1,32,32]{2,1,0:T(8,128)(2,1)S(1)}, u32[]{:S(2)}, u32[]{:S(2)}) collective-permute-start(bf16[1,32,32]{2,1,0:T(8,128)(2,1)S(1)} %get-tuple-element.517), channel_id=1, source_target_pairs={{16,0},{32,16},{48,32},{64,48},{80,64},{96,80},{112,96},{128,112},... | collective-permute-start | bytes 6152 | tf_op jit(solution)/shard_map/ppermute | solution.py:28
  22.0 9.5 %copy-start.7 = (s32[2,32,64]{2,1,0:T(8,128)S(1)}, s32[2,32,64]{2,1,0:T(8,128)}, u32[]{:S(2)}) copy-start(s32[2,32,64]{2,1,0:T(8,128)} %param.17) | copy-start | bytes 49156
  31.7 5.9 %collective-permute-start.2 = (bf16[1,32,1088]{2,1,0:T(8,128)(2,1)S(1)}, bf16[1,32,1088]{2,1,0:T(8,128)(2,1)S(1)}, u32[]{:S(2)}, u32[]{:S(2)}) collective-permute-start(bf16[1,32,1088]{2,1,0:T(8,128)(2,1)S(1)} %concatenate.27), channel_id=1, source_target_pairs={{0,2},{2,4},{4,6},{6,8},{8,10},{10,12},{12,14},{1,3},{3,5},{5,7},{... | collective-permute-start | bytes 208904 | tf_op jit(solution)/shard_map/ppermute | solution.py:27
  35.7 5.7 %collective-permute-start.3 = (bf16[1,32,1088]{2,1,0:T(8,128)(2,1)S(1)}, bf16[1,32,1088]{2,1,0:T(8,128)(2,1)S(1)}, u32[]{:S(2)}, u32[]{:S(2)}) collective-permute-start(bf16[1,32,1088]{2,1,0:T(8,128)(2,1)S(1)} %concatenate.27), channel_id=1, source_target_pairs={{2,0},{4,2},{6,4},{8,6},{10,8},{12,10},{14,12},{3,1},{5,3},{7,5},{... | collective-permute-start | bytes 208904 | tf_op jit(solution)/shard_map/ppermute | solution.py:28
  117.8 0.7 copy-start.2
  117.8 14.9 %copy-start.6 = (bf16[2,64,64]{2,1,0:T(8,128)(2,1)S(1)}, bf16[2,64,64]{2,1,0:T(8,128)(2,1)}, u32[]{:S(2)}) copy-start(bf16[2,64,64]{2,1,0:T(8,128)(2,1)} %param.14) | copy-start | bytes 49156
  118.8 18.4 %copy-start = (f32[2,32,8,128]{1,3,2,0:T(8,128)}, f32[2,32,8,128]{1,3,2,0:T(8,128)S(1)}, u32[]{:S(2)}) copy-start(f32[2,32,8,128]{1,3,2,0:T(8,128)S(1)} %copy.83) | copy-start | bytes 786436
  119.1 7.6 %collective-permute-start.4 = (bf16[2,32,32]{1,2,0:T(8,128)(2,1)S(1)}, bf16[2,32,32]{1,2,0:T(8,128)(2,1)S(1)}, u32[]{:S(2)}, u32[]{:S(2)}) collective-permute-start(bf16[2,32,32]{1,2,0:T(8,128)(2,1)S(1)} %get-tuple-element.508), channel_id=1, source_target_pairs={{0,16},{16,32},{32,48},{48,64},{64,80},{80,96},{96,112},{112,128},... | collective-permute-start | bytes 12296 | tf_op jit(solution)/shard_map/ppermute | solution.py:27
  121.0 6.3 %collective-permute-start.5 = (bf16[2,32,32]{1,2,0:T(8,128)(2,1)S(1)}, bf16[2,32,32]{1,2,0:T(8,128)(2,1)S(1)}, u32[]{:S(2)}, u32[]{:S(2)}) collective-permute-start(bf16[2,32,32]{1,2,0:T(8,128)(2,1)S(1)} %get-tuple-element.507), channel_id=1, source_target_pairs={{16,0},{32,16},{48,32},{64,48},{80,64},{96,80},{112,96},{128,112},... | collective-permute-start | bytes 12296 | tf_op jit(solution)/shard_map/ppermute | solution.py:28
  127.6 10.0 %collective-permute-start.6 = (bf16[2,32,1088]{2,1,0:T(8,128)(2,1)S(1)}, bf16[2,32,1088]{2,1,0:T(8,128)(2,1)S(1)}, u32[]{:S(2)}, u32[]{:S(2)}) collective-permute-start(bf16[2,32,1088]{2,1,0:T(8,128)(2,1)S(1)} %concatenate.30), channel_id=1, source_target_pairs={{0,2},{2,4},{4,6},{6,8},{8,10},{10,12},{12,14},{1,3},{3,5},{5,7},{... | collective-permute-start | bytes 417800 | tf_op jit(solution)/shard_map/ppermute | solution.py:27
  130.6 7.0 %collective-permute-start.7 = (bf16[2,32,1088]{2,1,0:T(8,128)(2,1)S(1)}, bf16[2,32,1088]{2,1,0:T(8,128)(2,1)S(1)}, u32[]{:S(2)}, u32[]{:S(2)}) collective-permute-start(bf16[2,32,1088]{2,1,0:T(8,128)(2,1)S(1)} %concatenate.30), channel_id=1, source_target_pairs={{2,0},{4,2},{6,4},{8,6},{10,8},{12,10},{14,12},{3,1},{5,3},{7,5},{... | collective-permute-start | bytes 417800 | tf_op jit(solution)/shard_map/ppermute | solution.py:28
  139.1 79.6 %copy-start.8 = (s32[32]{0:T(128)S(1)}, s32[32]{0:T(128)}, u32[]{:S(2)}) copy-start(s32[32]{0:T(128)} %param.16) | copy-start | bytes 388
  139.1 79.6 %copy-start.9 = (s32[32]{0:T(128)S(1)}, s32[32]{0:T(128)}, u32[]{:S(2)}) copy-start(s32[32]{0:T(128)} %param.15) | copy-start | bytes 388
  218.6 69.6 %copy-start.4 = (f32[32,1024]{1,0:T(8,128)S(1)}, f32[32,1024]{1,0:T(8,128)}, u32[]{:S(2)}) copy-start(f32[32,1024]{1,0:T(8,128)} %param.13) | copy-start | bytes 393220
  219.5 10.4 %all-to-all-start = ((f32[2,32,1024]{2,1,0:T(8,128)}), f32[2,32,1024]{2,1,0:T(8,128)S(1)}, u32[]{:S(2)}, u32[]{:S(2)}) async-start(f32[2,32,1024]{2,1,0:T(8,128)} %broadcast_in_dim.13), calls=%async_computation | async-start | bytes 524288 | tf_op jit(solution)/shard_map/all_to_all | solution.py:39
  288.4 7.4 %collective-permute-start.8 = (bf16[1,32,32]{2,1,0:T(8,128)(2,1)S(1)}, bf16[1,32,32]{2,1,0:T(8,128)(2,1)S(1)}, u32[]{:S(2)}, u32[]{:S(2)}) collective-permute-start(bf16[1,32,32]{2,1,0:T(8,128)(2,1)S(1)} %get-tuple-element.516), channel_id=1, source_target_pairs={{0,16},{16,32},{32,48},{48,64},{64,80},{80,96},{96,112},{112,128},... | collective-permute-start | bytes 6152 | tf_op jit(solution)/shard_map/ppermute | solution.py:27
  292.0 4.7 %collective-permute-start.9 = (bf16[1,32,32]{2,1,0:T(8,128)(2,1)S(1)}, bf16[1,32,32]{2,1,0:T(8,128)(2,1)S(1)}, u32[]{:S(2)}, u32[]{:S(2)}) collective-permute-start(bf16[1,32,32]{2,1,0:T(8,128)(2,1)S(1)} %get-tuple-element.515), channel_id=1, source_target_pairs={{16,0},{32,16},{48,32},{64,48},{80,64},{96,80},{112,96},{128,112},... | collective-permute-start | bytes 6152 | tf_op jit(solution)/shard_map/ppermute | solution.py:28
  296.9 5.9 %collective-permute-start.10 = (bf16[1,32,1088]{2,1,0:T(8,128)(2,1)S(1)}, bf16[1,32,1088]{2,1,0:T(8,128)(2,1)S(1)}, u32[]{:S(2)}, u32[]{:S(2)}) collective-permute-start(bf16[1,32,1088]{2,1,0:T(8,128)(2,1)S(1)} %concatenate.33), channel_id=1, source_target_pairs={{0,2},{2,4},{4,6},{6,8},{8,10},{10,12},{12,14},{1,3},{3,5},{5,7},{... | collective-permute-start | bytes 208904 | tf_op jit(solution)/shard_map/ppermute | solution.py:27
  300.7 5.7 %collective-permute-start.11 = (bf16[1,32,1088]{2,1,0:T(8,128)(2,1)S(1)}, bf16[1,32,1088]{2,1,0:T(8,128)(2,1)S(1)}, u32[]{:S(2)}, u32[]{:S(2)}) collective-permute-start(bf16[1,32,1088]{2,1,0:T(8,128)(2,1)S(1)} %concatenate.33), channel_id=1, source_target_pairs={{2,0},{4,2},{6,4},{8,6},{10,8},{12,10},{14,12},{3,1},{5,3},{7,5},{... | collective-permute-start | bytes 208904 | tf_op jit(solution)/shard_map/ppermute | solution.py:28
  307.5 76.8 %copy-start.5 = (f32[2,32,1024]{2,1,0:T(8,128)S(1)}, f32[2,32,1024]{2,1,0:T(8,128)}, u32[]{:S(2)}) copy-start(f32[2,32,1024]{2,1,0:T(8,128)} %param.12) | copy-start | bytes 786436
  382.8 0.7 copy-start.3
  382.9 58.4 %copy-start.1 = (f32[2,32,8,128]{1,3,2,0:T(8,128)S(1)}, f32[2,32,8,128]{1,3,2,0:T(8,128)}, u32[]{:S(2)}) copy-start(f32[2,32,8,128]{1,3,2,0:T(8,128)} %copy-done) | copy-start | bytes 786436
where the time goes:
time: 455 us; the launch traced here: 448 us
  local copies, waits for them, and re-layouts  218 us (48%)
  blocking collectives  110 us (24%)
  starting transfers between devices  50.3 us (11%)
  matrix products  40.8 us (9%)
  waiting for transfers between devices  13.6 us (3%)
  other arithmetic  8.53 us (2%)
    while x168, local copies, waits for them, and re-layouts  162 us
    psum x10, blocking collectives, one_axis_at_a_time(): return functools.reduce(lax.psum, axes, array)  110 us
    dot_general x24, matrix products, group_turn(): jnp.einsum(pattern, stacked, band_rows, preferred_element_type=jnp.float32)  31.9 us
    ppermute x6, starting transfers between devices, padded_2(): after = lax.ppermute(leading, axis, down)  26.1 us
    another operation x24, local copies, waits for them, and re-layouts, group_turn(): jnp.stack([lax.dynamic_slice_in_dim(windows, first_row + offset, row_coun...  23.2 us
    ppermute x6, starting transfers between devices, padded_2(): before = lax.ppermute(last, axis, up)  20.4 us
    unnamed x33, local copies, waits for them, and re-layouts  16.2 us
    dynamic_slice x8, local copies, waits for them, and re-layouts, group_turn(): band_rows = lax.dynamic_slice_in_dim(band, first_row, GROUP_ROWS, 1)  10.2 us
  transfers between devices with their start and end apart: 13, of which 5 were waited for; matrix products, arithmetic and copies ran while one was open for 5% of the time, Pallas kernels for 0%

commit v1 on v0

v1 whole, which is shorter than its diff:
```python
import jax
import jax.numpy as jnp
from jax import lax
from jax.experimental import pallas as pl
from jax.experimental.pallas import tpu as pltpu
from jax.sharding import PartitionSpec as P

EPSILON = 1e-06
MESH = pl.DeviceIdType.MESH
F32 = jnp.float32
BF16 = jnp.bfloat16
LANES = 128
SUB = 8


def build(dwell_shape, influence_shape, words, az_count, rad_count, tool_count):
    tools, rows, width = dwell_shape
    extent = influence_shape[-1]
    tiles = width // LANES
    assert tiles == SUB and extent == 64 and rows == 32
    pairs = rows // 2
    field = rows * tiles
    steps = extent // 2 + 1
    group_count = rad_count * tool_count
    share = width // tool_count
    share_tiles = share // LANES

    def body(
        dwell_hbm,
        residual_hbm,
        influence_ref,
        start_ref,
        end_ref,
        bits_ref,
        dwell_out,
        residual_out,
        direction_out,
        natural,
        dwell_v,
        whole,
        masked,
        masked_edge,
        masked_edge_out,
        low_out,
        low_edge_out,
        low_in,
        low_edge_in,
        inside,
        allowed,
        head_adj,
        head_fwd,
        head_two,
        keep,
        band_adj,
        band_fwd,
        win_adj,
        win_fwd,
        acc,
        acc_fwd,
        gradient,
        grad_low,
        grad_edge_out,
        grad_in,
        grad_edge_in,
        part,
        part_in,
        removal,
        removal_edge_out,
        removal_edge,
        edge,
        gradient_new,
        dwell_res,
        residual_res,
        direction_res,
        msg,
        box_a,
        box_b,
        local_sem,
        halo_send,
        halo_recv,
        tool_sem,
        sum_send,
        sum_recv,
    ):
        az, rad, tool = lax.axis_index("az"), lax.axis_index("rad"), lax.axis_index("tool")
        lane = lax.broadcasted_iota(jnp.int32, (SUB, LANES), 1)
        sub = lax.broadcasted_iota(jnp.int32, (SUB, LANES), 0)
        left_half = lane < LANES // 2

        residual_copy = pltpu.make_async_copy(residual_hbm, natural, local_sem.at[0])
        residual_copy.start()
        dwell_copy = pltpu.make_async_copy(dwell_hbm, dwell_v, local_sem.at[1])
        dwell_copy.start()

        def at(dr, da):
            return {
                "az": lax.rem(az + da + az_count, az_count),
                "rad": rad + dr,
                "tool": tool,
            }

        def group_peer(step):
            peer = lax.rem(rad * tool_count + tool + step, group_count)
            return {"az": az, "rad": peer // tool_count, "tool": lax.rem(peer, tool_count)}

        def ring_peer(step):
            return {"az": lax.rem(az + step, az_count), "rad": rad, "tool": tool}

        has_up, has_down = rad > 0, rad < rad_count - 1

        barrier = pltpu.get_barrier_semaphore()

        def greet(peer):
            pl.semaphore_signal(barrier, inc=1, device_id=peer, device_id_type=MESH)

        @pl.loop(1, group_count)
        def _(step):
            greet(group_peer(step))

        @pl.loop(1, az_count)
        def _(step):
            greet(ring_peer(step))

        @pl.when(has_up)
        def _():
            greet(at(-1, -1))
            greet(at(-1, 1))

        @pl.when(has_down)
        def _():
            greet(at(1, -1))
            greet(at(1, 1))

        residual_copy.wait()
        for c in range(tiles):
            whole[pl.ds(c, rows, stride=tiles), :] = natural[:, c * LANES : (c + 1) * LANES]
        column = az * width + sub * LANES + lane

        @pl.loop(0, rows)
        def _(r):
            at_r = pl.ds(pl.multiple_of(r * tiles, tiles), tiles)
            valid = ((column >= start_ref[r]) & (column < end_ref[r])).astype(F32)
            inside[at_r, :] = valid
            masked[1, at_r, :] = valid * whole[at_r, :]

        low_out[...] = masked[1].astype(BF16)
        for side, tile in ((0, tiles - 1), (1, 0)):
            tile_of = masked[1, pl.ds(tile, rows, stride=tiles), :]
            masked_edge_out[side] = tile_of
            low_edge_out[side] = tile_of.astype(BF16)

        extra = 2 * (has_up.astype(jnp.int32) + has_down.astype(jnp.int32))
        pl.semaphore_wait(barrier, group_count + az_count - 2 + extra)

        def halo(phase, mid_src, mid_dst, edge_src, edge_dst):
            copies = []
            for d in (0, 2, 1):
                for side, da in ((1, 0), (0, 1), (2, -1)):
                    if d == 1 and side == 1:
                        continue
                    src = mid_src if side == 1 else edge_src.at[side // 2]
                    dst = mid_dst.at[d] if side == 1 else edge_dst.at[d, side // 2]
                    copy = pltpu.make_async_remote_copy(
                        src_ref=src,
                        dst_ref=dst,
                        send_sem=halo_send.at[phase, 3 * d + side],
                        recv_sem=halo_recv.at[phase, 3 * d + side],
                        device_id=at(1 - d, da),
                        device_id_type=MESH,
                    )
                    copies.append((d, copy))

            def start():
                for d, copy in copies:
                    if d == 1:
                        copy.start()
                    else:
                        pl.when(has_down if d == 0 else has_up)(copy.start)

            def wait_recv():
                for d, copy in copies:
                    if d == 1:
                        copy.wait_recv()
                    else:
                        pl.when(has_up if d == 0 else has_down)(copy.wait_recv)

            def wait_send():
                for d, copy in copies:
                    if d == 1:
                        copy.wait_send()
                    else:
                        pl.when(has_down if d == 0 else has_up)(copy.wait_send)

            return start, wait_recv, wait_send

        first_halo = halo(0, low_out, low_in, low_edge_out, low_edge_in)
        masked_halo = halo(1, masked.at[1], masked, masked_edge_out, masked_edge)
        grad_halo = halo(2, grad_low, grad_in, grad_edge_out, grad_edge_in)
        removal_halo = halo(3, removal.at[1], removal, removal_edge_out, removal_edge)

        first_halo[0]()

        j_of = lax.broadcasted_iota(jnp.int32, (extent, LANES), 0)
        l_of = lax.broadcasted_iota(jnp.int32, (extent, LANES), 1)

        def spread(rows_of, where_j):
            return jnp.dot(rows_of, (l_of == where_j).astype(BF16), preferred_element_type=F32)

        head_adj[...] = spread(influence_ref[0], j_of) + spread(influence_ref[1], extent + j_of)
        head_fwd[...] = jnp.zeros_like(head_fwd)
        head_two[...] = jnp.zeros_like(head_two)
        for t in range(tools):
            head_fwd[t, 0:extent, :] = spread(influence_ref[t], extent - 1 - j_of)
            head_two[t, 1 : extent + 1, :] = spread(influence_ref[t], 2 * extent - 1 - j_of)
        head_fwd[...] = head_fwd[...] + head_two[...]
        c_of = lax.broadcasted_iota(jnp.int32, (LANES, LANES), 0)
        o_of = lax.broadcasted_iota(jnp.int32, (LANES, LANES), 1)
        low_side = o_of < extent
        off = o_of - c_of
        adj_keep = (low_side & (off >= -extent) & (off < 0)) | (~low_side & (off >= 0) & (off < extent))
        fwd_keep = (low_side & (off > -extent) & (off <= 0)) | (~low_side & (off > 0) & (off <= extent))
        keep[0] = adj_keep.astype(F32)
        keep[1] = fwd_keep.astype(F32)
        blank = jnp.zeros((LANES, LANES), BF16)
        band_adj[0:LANES, :] = blank
        band_adj[LANES : 2 * LANES, :] = blank
        band_adj[(extent + 2) * LANES : (extent + 3) * LANES, :] = blank
        for t in range(tools):
            band_fwd[t, (extent + 1) * LANES : (extent + 2) * LANES, :] = blank

        def toeplitz(head, shift, which):
            square = jnp.broadcast_to(head, (LANES, LANES))
            turned = pltpu.roll(square, shift, axis=1, stride=1, stride_axis=0)
            return (turned * keep[which]).astype(BF16)

        @pl.loop(0, extent)
        def _(i):
            at_i = pl.ds(pl.multiple_of((extent + 1 - i) * LANES, LANES), LANES)
            band_adj[at_i, :] = toeplitz(head_adj[pl.ds(i, 1), :], extent, 0)

        k_of = lax.broadcasted_iota(jnp.int32, (words, LANES), 0)
        b_of = lax.broadcasted_iota(jnp.int32, (words, LANES), 1)
        word = bits_ref[...].reshape(tools * rows, words)
        low_byte = (word & 255).astype(F32).astype(BF16)
        high_byte = (word >> 8).astype(F32).astype(BF16)
        for c in range(tiles):
            mine = k_of == c * (LANES // 16) + b_of // 16
            upper = b_of % 16 >= 8
            byte = jnp.dot(low_byte, (mine & ~upper).astype(BF16), preferred_element_type=F32)
            byte += jnp.dot(high_byte, (mine & upper).astype(BF16), preferred_element_type=F32)
            bit_at = lax.broadcasted_iota(jnp.int32, byte.shape, 1) % 8
            allowed[pl.ds(c, tools * rows, stride=tiles), :] = (
                (byte.astype(jnp.int32) >> bit_at) & 1
            ).astype(F32)

        def assemble(target, d, two_rows):
            @pl.loop(0, pairs)
            def _(m):
                both = two_rows(m)
                for a in range(2):
                    row = both[a * tiles : (a + 1) * tiles]
                    before = jnp.broadcast_to(edge[0, pl.ds(2 * m + a, 1), :], (SUB, LANES))
                    after = jnp.broadcast_to(edge[1, pl.ds(2 * m + a, 1), :], (SUB, LANES))
                    prior = jnp.where(sub == 0, before, pltpu.roll(row, 1, axis=0))
                    later = jnp.where(sub == SUB - 1, after, pltpu.roll(row, SUB - 1, axis=0))
                    even = pltpu.roll(jnp.where(lane >= 96, prior, row), 32, axis=1)
                    odd = pltpu.roll(jnp.where(lane < 32, later, row), 96, axis=1)
                    target[
                        pl.ds(pl.multiple_of((pairs * d + m) * 16, 16), 16),
                        a * LANES : (a + 1) * LANES,
                    ] = jnp.concatenate([even, odd], axis=0).astype(BF16)

        def at_pair(m):
            return pl.ds(pl.multiple_of(m * 2 * tiles, 2 * tiles), 2 * tiles)

        def fill_blank(target, d):
            target[d * pairs * 16 : (d + 1) * pairs * 16, :] = jnp.zeros((pairs * 16, 2 * LANES), BF16)

        def over_blocks(block, blank_of=None):
            block(1)
            for d, there in ((0, has_up), (2, has_down)):
                pl.when(there)(lambda d=d: block(d))
                if blank_of is not None:
                    pl.when(jnp.logical_not(there))(lambda d=d: blank_of(d))

        def adjoint(out):
            acc[...] = jnp.zeros_like(acc)

            @pl.loop(0, steps // 3)
            def _(kk):
                lhs = jnp.concatenate(
                    [
                        win_adj[pl.ds(pl.multiple_of((3 * kk + u) * 16, 16), pairs * 16), :]
                        for u in range(3)
                    ],
                    axis=1,
                )
                first = pl.multiple_of(6 * kk * LANES, LANES)
                rhs = jnp.concatenate(
                    [
                        band_adj[pl.ds(first + LANES, 6 * LANES), :],
                        band_adj[pl.ds(first, 6 * LANES), :],
                    ],
                    axis=1,
                )
                acc[...] += jnp.dot(lhs, rhs, preferred_element_type=F32)

            def finish(m, total):
                for b in range(2):
                    cols = slice(b * LANES, (b + 1) * LANES)
                    even = acc[pl.ds(pl.multiple_of(m * 16, 16), 8), cols]
                    odd = acc[pl.ds(pl.multiple_of(m * 16 + 8, 8), 8), cols]
                    values = (
                        jnp.where(left_half, even, pltpu.roll(odd, 64, axis=1)),
                        jnp.where(left_half, pltpu.roll(even, 64, axis=1), odd),
                    )
                    for t in range(tools):
                        at_r = pl.ds(pl.multiple_of((t * rows + 2 * m + b) * tiles, tiles), tiles)
                        value = allowed[at_r, :] * values[t]
                        out[at_r, :] = value
                        total = total + value * value
                return total

            return lax.fori_loop(0, pairs, finish, jnp.zeros((SUB, LANES), F32))

        def sum_stage(which, source, box, count, peer_of):
            def copy_to(step):
                return pltpu.make_async_remote_copy(
                    src_ref=msg.at[source],
                    dst_ref=box.at[step - 1],
                    send_sem=sum_send.at[which],
                    recv_sem=sum_recv.at[which],
                    device_id=peer_of(step),
                    device_id_type=MESH,
                )

            @pl.loop(1, count)
            def _(step):
                copy_to(step).start()

            all_of = pltpu.make_async_remote_copy(
                src_ref=box,
                dst_ref=box,
                send_sem=sum_send.at[which],
                recv_sem=sum_recv.at[which],
                device_id=peer_of(1),
                device_id_type=MESH,
            )
            return all_of

        def total_of(first, side_work):
            stage = sum_stage(first, first, box_a.at[first // 2], group_count, group_peer)
            side_work()
            stage.wait_recv()
            msg[first + 1] = msg[first] + jnp.sum(box_a[first // 2], axis=0)
            other = sum_stage(first + 1, first + 1, box_b.at[first // 2], az_count, ring_peer)
            other.wait_recv()
            everything = msg[first + 1] + jnp.sum(box_b[first // 2], axis=0)
            return jnp.sum(everything, axis=1, keepdims=True), (stage, other)

        first_halo[1]()

        def first_block(d):
            if d == 1:
                edge[...] = low_edge_in[1].astype(F32)
                assemble(win_adj, 1, lambda m: masked[1, at_pair(m), :])
            else:
                edge[...] = low_edge_in[d].astype(F32)
                assemble(win_adj, d, lambda m: low_in[d, at_pair(m), :].astype(F32))

        over_blocks(first_block, lambda d: fill_blank(win_adj, d))
        masked_halo[0]()
        gamma_part = adjoint(gradient)
        grad_low[...] = gradient[...].astype(BF16)
        for side, tile in ((0, tiles - 1), (1, 0)):
            grad_edge_out[side] = gradient[pl.ds(tile, tools * rows, stride=tiles), :].astype(BF16)
        grad_halo[0]()

        for t in range(tools):

            @pl.loop(0, extent + 1)
            def _(q, t=t):
                at_q = pl.ds(pl.multiple_of(q * LANES, LANES), LANES)
                band_fwd[t, at_q, :] = toeplitz(head_fwd[t, pl.ds(q, 1), :], extent + 1, 1)

        grad_halo[1]()

        def grad_block(d):
            for t in range(tools):
                edge[...] = grad_edge_in[d, :, t * rows : (t + 1) * rows, :].astype(F32)
                first = t * field
                if d == 1:
                    assemble(win_fwd.at[t], 1, lambda m, first=first: gradient[pl.ds(pl.multiple_of(first + m * 16, 16), 16), :])
                else:
                    assemble(
                        win_fwd.at[t],
                        d,
                        lambda m, first=first: grad_in[
                            d, pl.ds(pl.multiple_of(first + m * 16, 16), 16), :
                        ].astype(F32),
                    )

        def grad_blank(d):
            for t in range(tools):
                fill_blank(win_fwd.at[t], d)

        over_blocks(grad_block, grad_blank)

        acc_fwd[...] = jnp.zeros_like(acc_fwd)

        @pl.loop(0, steps // 3)
        def _(kk):
            lhs = jnp.concatenate(
                [
                    win_fwd[t, pl.ds(pl.multiple_of((3 * kk + u) * 16, 16), pairs * 16), :]
                    for t in range(tools)
                    for u in range(3)
                ],
                axis=1,
            )
            first = pl.multiple_of(6 * kk * LANES, LANES)
            rhs = jnp.concatenate(
                [band_fwd[t, pl.ds(first, 6 * LANES), :] for t in range(tools)], axis=0
            )
            acc_fwd[...] += jnp.dot(lhs, rhs, preferred_element_type=F32)

        @pl.loop(0, pairs)
        def _(m):
            even = acc_fwd[pl.ds(pl.multiple_of(m * 16, 16), 8), :]
            odd = acc_fwd[pl.ds(pl.multiple_of(m * 16 + 8, 8), 8), :]
            top = jnp.where(left_half, even, pltpu.roll(odd, 64, axis=1))
            low = jnp.where(left_half, pltpu.roll(even, 64, axis=1), odd)
            at_m = at_pair(m)
            part[at_m, :] = inside[at_m, :] * jnp.concatenate([top, low], axis=0)

        tool_copies = []
        for step in range(1, tool_count):
            tool_copies.append(
                pltpu.make_async_remote_copy(
                    src_ref=part,
                    dst_ref=part_in.at[step - 1],
                    send_sem=tool_sem.at[0, step - 1],
                    recv_sem=tool_sem.at[1, step - 1],
                    device_id={"az": az, "rad": rad, "tool": lax.rem(tool + step, tool_count)},
                    device_id_type=MESH,
                )
            )
        for copy in tool_copies:
            copy.start()
        for copy in tool_copies:
            copy.wait_recv()

        def join(m, total):
            at_m = at_pair(m)
            value = part[at_m, :]
            for step in range(1, tool_count):
                value = value + part_in[step - 1, at_m, :]
            removal[1, at_m, :] = value
            return total + value[:SUB] * value[:SUB] + value[SUB:] * value[SUB:]

        curvature_part = lax.fori_loop(0, pairs, join, jnp.zeros((SUB, LANES), F32))
        for side, tile in ((0, tiles - 1), (1, 0)):
            removal_edge_out[side] = removal[1, pl.ds(tile, rows, stride=tiles), :]
        msg[0] = jnp.concatenate(
            [
                jnp.sum(gamma_part, axis=0, keepdims=True),
                jnp.sum(curvature_part, axis=0, keepdims=True),
            ],
            axis=0,
        )

        def beside():
            removal_halo[0]()
            masked_halo[1]()
            removal_halo[1]()
            dwell_copy.wait()

        sums, stages = total_of(0, beside)
        gamma = sums[0:1]
        curvature = sums[1:2] * (1.0 / tool_count)
        step_size = gamma / (curvature + EPSILON)

        def second_block(d):
            edge[...] = masked_edge[d] - step_size * removal_edge[d]
            assemble(
                win_adj, d, lambda m: masked[d, at_pair(m), :] - step_size * removal[d, at_pair(m), :]
            )

        over_blocks(second_block)
        new_part = adjoint(gradient_new)
        new_row = jnp.sum(new_part, axis=0, keepdims=True)
        msg[2] = jnp.concatenate([new_row, new_row], axis=0)

        dwell_store = pltpu.make_async_copy(dwell_res, dwell_out, local_sem.at[2])
        residual_store = pltpu.make_async_copy(residual_res, residual_out, local_sem.at[3])
        direction_store = pltpu.make_async_copy(direction_res, direction_out, local_sem.at[4])

        def outputs():
            for t in range(tools):
                for c in range(tiles):
                    cols = slice(c * LANES, (c + 1) * LANES)
                    step_of = gradient[pl.ds(t * field + c, rows, stride=tiles), :]
                    dwell_res[t, :, cols] = dwell_v[t, :, cols] + step_size * step_of
            dwell_store.start()
            for c in range(share_tiles):
                from_c = pl.ds(tool * share_tiles + c, rows, stride=tiles)
                residual_res[:, c * LANES : (c + 1) * LANES] = (
                    whole[from_c, :] - step_size * removal[1, from_c, :]
                )
            residual_store.start()

        new_sums, new_stages = total_of(2, outputs)
        ratio = new_sums[0:1] / (gamma + EPSILON)
        for t in range(tools):
            for c in range(tiles):
                cols = slice(c * LANES, (c + 1) * LANES)
                from_c = pl.ds(t * field + c, rows, stride=tiles)
                direction_res[t, :, cols] = gradient_new[from_c, :] + ratio * gradient[from_c, :]
        direction_store.start()

        for phase in (first_halo, masked_halo, grad_halo, removal_halo):
            phase[2]()
        for copy in tool_copies:
            copy.wait_send()
        for stage in stages + new_stages:
            stage.wait_send()
        dwell_store.wait()
        residual_store.wait()
        direction_store.wait()

    any_spec = pl.BlockSpec(memory_space=pl.ANY)
    vmem_spec = pl.BlockSpec(memory_space=pltpu.VMEM)
    smem_spec = pl.BlockSpec(memory_space=pltpu.SMEM)
    scratch = [
        ((rows, width), F32),
        (dwell_shape, F32),
        ((field, LANES), F32),
        ((3, field, LANES), F32),
        ((3, 2, rows, LANES), F32),
        ((2, rows, LANES), F32),
        ((field, LANES), BF16),
        ((2, rows, LANES), BF16),
        ((3, field, LANES), BF16),
        ((3, 2, rows, LANES), BF16),
        ((field, LANES), F32),
        ((tools * field, LANES), F32),
        ((extent, LANES), F32),
        ((tools, extent + 8, LANES), F32),
        ((tools, extent + 8, LANES), F32),
        ((2, LANES, LANES), F32),
        (((extent + 3) * LANES, LANES), BF16),
        ((tools, (extent + 2) * LANES, LANES), BF16),
        ((3 * pairs * 16, 2 * LANES), BF16),
        ((tools, 3 * pairs * 16, 2 * LANES), BF16),
        ((pairs * 16, 2 * LANES), F32),
        ((pairs * 16, LANES), F32),
        ((tools * field, LANES), F32),
        ((tools * field, LANES), BF16),
        ((2, tools * rows, LANES), BF16),
        ((3, tools * field, LANES), BF16),
        ((3, 2, tools * rows, LANES), BF16),
        ((field, LANES), F32),
        ((tool_count - 1, field, LANES), F32),
        ((3, field, LANES), F32),
        ((2, rows, LANES), F32),
        ((3, 2, rows, LANES), F32),
        ((2, rows, LANES), F32),
        ((tools * field, LANES), F32),
        (dwell_shape, F32),
        ((rows, share), F32),
        (dwell_shape, F32),
        ((4, 2, LANES), F32),
        ((2, group_count - 1, 2, LANES), F32),
        ((2, az_count - 1, 2, LANES), F32),
    ]
    return pl.pallas_call(
        body,
        out_shape=(
            jax.ShapeDtypeStruct(dwell_shape, F32),
            jax.ShapeDtypeStruct((rows, share), F32),
            jax.ShapeDtypeStruct(dwell_shape, F32),
        ),
        in_specs=[any_spec, any_spec, vmem_spec, smem_spec, smem_spec, vmem_spec],
        out_specs=(any_spec, any_spec, any_spec),
        scratch_shapes=[pltpu.VMEM(shape, dtype) for shape, dtype in scratch]
        + [
            pltpu.SemaphoreType.DMA((5,)),
            pltpu.SemaphoreType.DMA((4, 9)),
            pltpu.SemaphoreType.DMA((4, 9)),
            pltpu.SemaphoreType.DMA((2, max(tool_count - 1, 1))),
            pltpu.SemaphoreType.DMA((4,)),
            pltpu.SemaphoreType.DMA((4,)),
        ],
        compiler_params=pltpu.CompilerParams(
            collective_id=0, has_side_effects=True, vmem_limit_bytes=40 * 1024 * 1024
        ),
        name="cgls",
    )


def solution(mesh):
    def per_device(dwell, residual, influence, cycle_start, cycle_end, allowed_bits):
        call = build(
            dwell.shape,
            influence.shape,
            allowed_bits.shape[-1],
            mesh.shape["az"],
            mesh.shape["rad"],
            mesh.shape["tool"],
        )
        return call(dwell, residual, influence, cycle_start, cycle_end, allowed_bits)

    in_specs = (
        P("tool", "rad", "az"),
        P("rad", "az"),
        P("tool", None, None),
        P("rad"),
        P("rad"),
        P("tool", "rad", "az"),
    )
    out_specs = (P("tool", "rad", "az"), P("rad", ("az", "tool")), P("tool", "rad", "az"))
    return jax.shard_map(
        per_device, mesh=mesh, in_specs=in_specs, out_specs=out_specs, check_vma=False
    )
```

time: 455 us -> 104 us (0.23); the launches traced: 448 us -> 104 us
  local copies, waits for them, and re-layouts: 218 us -> 6.71 us
  blocking collectives: 110 us -> 0 us
  Pallas kernels: 0 us -> 96.7 us
  starting transfers between devices: 50.3 us -> 0 us
  matrix products: 40.8 us -> 0 us
  waiting for transfers between devices: 13.6 us -> 0 us
  other arithmetic: 8.53 us -> 0 us
    while x170 -> x0, local copies, waits for them, and re-layouts: 163 us -> none
    psum x10 -> x0, blocking collectives: 110 us -> none  [one_axis_at_a_time(): return functools.reduce(lax.psum, axes, array)]
    pallas_call x0 -> x1, Pallas kernels: none -> 96.7 us  [per_device(): call(dwell, residual, influence, cycle_start, cycle_end, allowed_bits)]
    ppermute x12 -> x0, starting transfers between devices: 46.4 us -> none  [the longest x6 26.1 us: padded_2(): after = lax.ppermute(leading, axis, down)]
    dot_general x26 -> x0, matrix products: 40.8 us -> none  [the longest x24 31.9 us: group_turn(): jnp.einsum(pattern, stacked, band_rows, preferred_element_type=jnp.float32)]
    another operation x24 -> x0, local copies, waits for them, and re-layouts: 23.2 us -> none  [group_turn(): jnp.stack([lax.dynamic_slice_in_dim(windows, first_row + offset, row_coun...]
    dynamic_slice x9 -> x0, local copies, waits for them, and re-layouts: 10.8 us -> none  [the longest x8 10.2 us: group_turn(): band_rows = lax.dynamic_slice_in_dim(band, first_row, GROUP_ROWS, 1)]
    unnamed x33 -> x15, local copies, waits for them, and re-layouts: 16.2 us -> 6.71 us
  transfers between devices with their start and end apart: 13 -> 0, of which waited for: 5 -> 0; matrix products, arithmetic and copies ran while one was open for 5% -> 0% of each run, Pallas kernels for 0% -> 0%
where the time goes in v1:
time: 104 us
  Pallas kernels  96.7 us (93%)
  local copies, waits for them, and re-layouts  6.71 us (6%)
    pallas_call x1, Pallas kernels, per_device(): call(dwell, residual, influence, cycle_start, cycle_end, allowed_bits)  96.7 us
    unnamed x15, local copies, waits for them, and re-layouts  6.71 us

profile of v1, /device:TPU:1, one launch (start us, length us, event | category | flops | bytes accessed | tf_op | source)
XLA Modules:
  0.0 104.0 jit_solution(9963678578319636650)
XLA Ops:
  0.6 0.0 copy-start
  0.6 0.9 copy-done
  1.6 0.0 copy-start.1
  1.6 0.9 copy-done.1
  2.5 0.0 copy-start.2
  2.5 0.8 copy-done.2
  3.2 0.0 copy-start.3
  3.2 0.8 copy-done.3
  4.0 0.0 copy-start.4
  4.0 0.7 copy-done.4
  4.7 0.0 copy-start.5
  4.7 0.7 copy-done.5
  5.3 96.7 %cgls.1 = (f32[2,32,1024]{2,1,0:T(8,128)S(1)}, f32[32,512]{1,0:T(8,128)S(1)}, f32[2,32,1024]{2,1,0:T(8,128)S(1)}) custom-call(f32[2,32,1024]{2,1,0:T(8,128)S(1)} %copy-done, f32[32,1024]{1,0:T(8,128)S(1)} %copy-done.1, bf16[2,64,64]{2,1,0:T(8,128)(2,1)S(1)} %copy-done.2, s32[32]{0:T(128)S(1)} %copy-done.4, s32[32]{0:T(128)S(1)} %copy-done.5, ...), custom_call_target="tpu_custom_call" | custom-call | tf_op jit(solution)/shard_map/cgls/pallas_call | solution.py:611
  102.0 0.7 copy.12
  102.7 0.6 copy.13
  103.3 0.7 copy.14
Async XLA Ops:
  0.6 1.0 copy-start
  1.6 0.9 copy-start.1
  2.5 0.8 copy-start.2
  3.2 0.8 copy-start.3
  4.0 0.7 copy-start.4
  4.7 0.7 copy-start.5

commit v2 on v1

--- a/solution.py
+++ b/solution.py
@@ -21,20 +21,27 @@
     pairs = rows // 2
     field = rows * tiles
     steps = extent // 2 + 1
-    group_count = rad_count * tool_count
+    plane_count = 2 * rad_count * tool_count
+    line_count = az_count // 2
+    for count in (az_count, rad_count, tool_count):
+        assert count & (count - 1) == 0
     share = width // tool_count
     share_tiles = share // LANES
 
     def body(
         dwell_hbm,
         residual_hbm,
+        influence_hbm,
+        start_hbm,
+        end_hbm,
+        bits_hbm,
+        dwell_out,
+        residual_out,
+        direction_out,
         influence_ref,
         start_ref,
         end_ref,
         bits_ref,
-        dwell_out,
-        residual_out,
-        direction_out,
         natural,
         dwell_v,
         whole,
@@ -88,9 +95,13 @@
         left_half = lane < LANES // 2
 
         residual_copy = pltpu.make_async_copy(residual_hbm, natural, local_sem.at[0])
-        residual_copy.start()
+        start_copy = pltpu.make_async_copy(start_hbm, start_ref, local_sem.at[5])
+        end_copy = pltpu.make_async_copy(end_hbm, end_ref, local_sem.at[6])
+        influence_copy = pltpu.make_async_copy(influence_hbm, influence_ref, local_sem.at[7])
+        bits_copy = pltpu.make_async_copy(bits_hbm, bits_ref, local_sem.at[8])
         dwell_copy = pltpu.make_async_copy(dwell_hbm, dwell_v, local_sem.at[1])
-        dwell_copy.start()
+        for copy in (residual_copy, start_copy, end_copy, influence_copy, bits_copy, dwell_copy):
+            copy.start()
 
         def at(dr, da):
             return {
@@ -99,12 +110,15 @@
                 "tool": tool,
             }
 
-        def group_peer(step):
-            peer = lax.rem(rad * tool_count + tool + step, group_count)
-            return {"az": az, "rad": peer // tool_count, "tool": lax.rem(peer, tool_count)}
-
-        def ring_peer(step):
-            return {"az": lax.rem(az + step, az_count), "rad": rad, "tool": tool}
+        def plane_peer(step):
+            return {
+                "az": az ^ (step % 2),
+                "rad": rad ^ (step // (2 * tool_count)),
+                "tool": tool ^ (step // 2 % tool_count),
+            }
+
+        def line_peer(step):
+            return {"az": az ^ (2 * step), "rad": rad, "tool": tool}
 
         has_up, has_down = rad > 0, rad < rad_count - 1
 
@@ -113,30 +127,29 @@
         def greet(peer):
             pl.semaphore_signal(barrier, inc=1, device_id=peer, device_id_type=MESH)
 
-        @pl.loop(1, group_count)
-        def _(step):
-            greet(group_peer(step))
-
-        @pl.loop(1, az_count)
-        def _(step):
-            greet(ring_peer(step))
+        for step in range(1, plane_count):
+            greet(plane_peer(step))
+        for step in range(1, line_count):
+            greet(line_peer(step))
+        outer = 1 - 2 * (1 - lax.rem(az, 2))
+        greet(at(0, outer))
 
         @pl.when(has_up)
         def _():
-            greet(at(-1, -1))
-            greet(at(-1, 1))
+            greet(at(-1, outer))
 
         @pl.when(has_down)
         def _():
-            greet(at(1, -1))
-            greet(at(1, 1))
+            greet(at(1, outer))
 
         residual_copy.wait()
         for c in range(tiles):
             whole[pl.ds(c, rows, stride=tiles), :] = natural[:, c * LANES : (c + 1) * LANES]
+        start_copy.wait()
+        end_copy.wait()
         column = az * width + sub * LANES + lane
 
-        @pl.loop(0, rows)
+        @pl.loop(0, rows, unroll=4)
         def _(r):
             at_r = pl.ds(pl.multiple_of(r * tiles, tiles), tiles)
             valid = ((column >= start_ref[r]) & (column < end_ref[r])).astype(F32)
@@ -149,8 +162,8 @@
             masked_edge_out[side] = tile_of
             low_edge_out[side] = tile_of.astype(BF16)
 
-        extra = 2 * (has_up.astype(jnp.int32) + has_down.astype(jnp.int32))
-        pl.semaphore_wait(barrier, group_count + az_count - 2 + extra)
+        extra = 1 + has_up.astype(jnp.int32) + has_down.astype(jnp.int32)
+        pl.semaphore_wait(barrier, plane_count + line_count - 2 + extra)
 
         def halo(phase, mid_src, mid_dst, edge_src, edge_dst):
             copies = []
@@ -200,6 +213,7 @@
 
         first_halo[0]()
 
+        influence_copy.wait()
         j_of = lax.broadcasted_iota(jnp.int32, (extent, LANES), 0)
         l_of = lax.broadcasted_iota(jnp.int32, (extent, LANES), 1)
 
@@ -233,13 +247,14 @@
             turned = pltpu.roll(square, shift, axis=1, stride=1, stride_axis=0)
             return (turned * keep[which]).astype(BF16)
 
-        @pl.loop(0, extent)
+        @pl.loop(0, extent, unroll=4)
         def _(i):
             at_i = pl.ds(pl.multiple_of((extent + 1 - i) * LANES, LANES), LANES)
             band_adj[at_i, :] = toeplitz(head_adj[pl.ds(i, 1), :], extent, 0)
 
         k_of = lax.broadcasted_iota(jnp.int32, (words, LANES), 0)
         b_of = lax.broadcasted_iota(jnp.int32, (words, LANES), 1)
+        bits_copy.wait()
         word = bits_ref[...].reshape(tools * rows, words)
         low_byte = (word & 255).astype(F32).astype(BF16)
         high_byte = (word >> 8).astype(F32).astype(BF16)
@@ -254,7 +269,7 @@
             ).astype(F32)
 
         def assemble(target, d, two_rows):
-            @pl.loop(0, pairs)
+            @pl.loop(0, pairs, unroll=4)
             def _(m):
                 both = two_rows(m)
                 for a in range(2):
@@ -321,7 +336,7 @@
                         total = total + value * value
                 return total
 
-            return lax.fori_loop(0, pairs, finish, jnp.zeros((SUB, LANES), F32))
+            return lax.fori_loop(0, pairs, finish, jnp.zeros((SUB, LANES), F32), unroll=4)
 
         def sum_stage(which, source, box, count, peer_of):
             def copy_to(step):
@@ -334,8 +349,7 @@
                     device_id_type=MESH,
                 )
 
-            @pl.loop(1, count)
-            def _(step):
+            for step in range(1, count):
                 copy_to(step).start()
 
             all_of = pltpu.make_async_remote_copy(
@@ -349,11 +363,11 @@
             return all_of
 
         def total_of(first, side_work):
-            stage = sum_stage(first, first, box_a.at[first // 2], group_count, group_peer)
+            stage = sum_stage(first, first, box_a.at[first // 2], plane_count, plane_peer)
             side_work()
             stage.wait_recv()
             msg[first + 1] = msg[first] + jnp.sum(box_a[first // 2], axis=0)
-            other = sum_stage(first + 1, first + 1, box_b.at[first // 2], az_count, ring_peer)
+            other = sum_stage(first + 1, first + 1, box_b.at[first // 2], line_count, line_peer)
             other.wait_recv()
             everything = msg[first + 1] + jnp.sum(box_b[first // 2], axis=0)
             return jnp.sum(everything, axis=1, keepdims=True), (stage, other)
@@ -378,7 +392,7 @@
 
         for t in range(tools):
 
-            @pl.loop(0, extent + 1)
+            @pl.loop(0, extent + 1, unroll=5)
             def _(q, t=t):
                 at_q = pl.ds(pl.multiple_of(q * LANES, LANES), LANES)
                 band_fwd[t, at_q, :] = toeplitz(head_fwd[t, pl.ds(q, 1), :], extent + 1, 1)
@@ -424,7 +438,7 @@
             )
             acc_fwd[...] += jnp.dot(lhs, rhs, preferred_element_type=F32)
 
-        @pl.loop(0, pairs)
+        @pl.loop(0, pairs, unroll=4)
         def _(m):
             even = acc_fwd[pl.ds(pl.multiple_of(m * 16, 16), 8), :]
             odd = acc_fwd[pl.ds(pl.multiple_of(m * 16 + 8, 8), 8), :]
@@ -458,7 +472,7 @@
             removal[1, at_m, :] = value
             return total + value[:SUB] * value[:SUB] + value[SUB:] * value[SUB:]
 
-        curvature_part = lax.fori_loop(0, pairs, join, jnp.zeros((SUB, LANES), F32))
+        curvature_part = lax.fori_loop(0, pairs, join, jnp.zeros((SUB, LANES), F32), unroll=4)
         for side, tile in ((0, tiles - 1), (1, 0)):
             removal_edge_out[side] = removal[1, pl.ds(tile, rows, stride=tiles), :]
         msg[0] = jnp.concatenate(
@@ -528,9 +542,7 @@
         residual_store.wait()
         direction_store.wait()
 
-    any_spec = pl.BlockSpec(memory_space=pl.ANY)
-    vmem_spec = pl.BlockSpec(memory_space=pltpu.VMEM)
-    smem_spec = pl.BlockSpec(memory_space=pltpu.SMEM)
+    hbm_spec = pl.BlockSpec(memory_space=pltpu.HBM)
     scratch = [
         ((rows, width), F32),
         (dwell_shape, F32),
@@ -570,8 +582,8 @@
         ((rows, share), F32),
         (dwell_shape, F32),
         ((4, 2, LANES), F32),
-        ((2, group_count - 1, 2, LANES), F32),
-        ((2, az_count - 1, 2, LANES), F32),
+        ((2, plane_count - 1, 2, LANES), F32),
+        ((2, line_count - 1, 2, LANES), F32),
     ]
     return pl.pallas_call(
         body,
@@ -580,11 +592,17 @@
             jax.ShapeDtypeStruct((rows, share), F32),
             jax.ShapeDtypeStruct(dwell_shape, F32),
         ),
-        in_specs=[any_spec, any_spec, vmem_spec, smem_spec, smem_spec, vmem_spec],
-        out_specs=(any_spec, any_spec, any_spec),
-        scratch_shapes=[pltpu.VMEM(shape, dtype) for shape, dtype in scratch]
+        in_specs=[hbm_spec] * 6,
+        out_specs=(hbm_spec,) * 3,
+        scratch_shapes=[
+            pltpu.VMEM(influence_shape, BF16),
+            pltpu.SMEM((rows,), jnp.int32),
+            pltpu.SMEM((rows,), jnp.int32),
+            pltpu.VMEM((tools, rows, words), jnp.int32),
+        ]
+        + [pltpu.VMEM(shape, dtype) for shape, dtype in scratch]
         + [
-            pltpu.SemaphoreType.DMA((5,)),
+            pltpu.SemaphoreType.DMA((9,)),
             pltpu.SemaphoreType.DMA((4, 9)),
             pltpu.SemaphoreType.DMA((4, 9)),
             pltpu.SemaphoreType.DMA((2, max(tool_count - 1, 1))),
@@ -592,10 +610,33 @@
             pltpu.SemaphoreType.DMA((4,)),
         ],
         compiler_params=pltpu.CompilerParams(
-            collective_id=0, has_side_effects=True, vmem_limit_bytes=40 * 1024 * 1024
+            collective_id=0, has_side_effects=True, vmem_limit_bytes=24 * 1024 * 1024
         ),
         name="cgls",
     )
+
+
+def hand_on(results):
+    count = len(results)
+
+    def body(*refs):
+        sem = refs[-1]
+        copies = [
+            pltpu.make_async_copy(refs[i], refs[count + i], sem.at[i]) for i in range(count)
+        ]
+        for copy in copies:
+            copy.start()
+        for copy in copies:
+            copy.wait()
+
+    return pl.pallas_call(
+        body,
+        out_shape=tuple(jax.ShapeDtypeStruct(x.shape, x.dtype) for x in results),
+        in_specs=[pl.BlockSpec(memory_space=pl.ANY)] * count,
+        out_specs=(pl.BlockSpec(memory_space=pltpu.HBM),) * count,
+        scratch_shapes=[pltpu.SemaphoreType.DMA((count,))],
+        name="hand_on",
+    )(*(pltpu.with_memory_space_constraint(x, pltpu.VMEM) for x in results))
 
 
 def solution(mesh):
@@ -608,7 +649,8 @@
             mesh.shape["rad"],
             mesh.shape["tool"],
         )
-        return call(dwell, residual, influence, cycle_start, cycle_end, allowed_bits)
+        given = (dwell, residual, influence, cycle_start, cycle_end, allowed_bits)
+        return hand_on(call(*(pltpu.with_memory_space_constraint(x, pltpu.HBM) for x in given)))
 
     in_specs = (
         P("tool", "rad", "az"),

time: 104 us -> 73 us (0.70)
  Pallas kernels: 96.7 us -> 72.2 us
  local copies, waits for them, and re-layouts: 6.71 us -> 0 us
    pallas_call x1 -> x2, Pallas kernels: 96.7 us -> 72.2 us  [the longest x1 71.4 us: per_device(): call(*(pltpu.with_memory_space_constraint(x, pltpu.HBM) for x in given))]
    unnamed x15 -> x0, local copies, waits for them, and re-layouts: 6.71 us -> none
where the time goes in v2:
time: 73 us; the launch traced here: 72.9 us
  Pallas kernels  72.2 us (99%)
    pallas_call x1, Pallas kernels, per_device(): call(*(pltpu.with_memory_space_constraint(x, pltpu.HBM) for x in given))  71.4 us

profile of v2, /device:TPU:1, one launch (start us, length us, event | category | flops | bytes accessed | tf_op | source)
XLA Modules:
  0.0 72.9 jit_solution(3732665574954374238)
XLA Ops:
  0.6 71.4 %cgls.1 = (f32[2,32,1024]{2,1,0:T(8,128)S(1)}, f32[32,512]{1,0:T(8,128)S(1)}, f32[2,32,1024]{2,1,0:T(8,128)S(1)}) custom-call(f32[2,32,1024]{2,1,0:T(8,128)} %dwell_hbm.1, f32[32,1024]{1,0:T(8,128)} %residual_hbm.1, bf16[2,64,64]{2,1,0:T(8,128)(2,1)} %influence_hbm.1, s32[32]{0:T(128)} %start_hbm.1, s32[32]{0:T(128)} %end_hbm.1, s32[2,32,64]{2,1,0:T(8,128)} %bits_hbm.1), custom_call_target="tpu_custom_call" | custom-call | tf_op jit(solution)/shard_map/cgls/pallas_call | solution.py:653
  72.0 0.8 %hand_on.1 = (f32[2,32,1024]{2,1,0:T(8,128)}, f32[32,512]{1,0:T(8,128)}, f32[2,32,1024]{2,1,0:T(8,128)}) custom-call(f32[2,32,1024]{2,1,0:T(8,128)S(1)} %get-tuple-element.6.refs_0_, f32[32,512]{1,0:T(8,128)S(1)} %get-tuple-element.7.refs_1_, f32[2,32,1024]{2,1,0:T(8,128)S(1)} %get-tuple-element.8.refs_2_), custom_call_target="tpu_custom_call" | custom-call | tf_op jit(solution)/shard_map/hand_on/pallas_call | solution.py:632

commit v3 on v2

--- a/solution.py
+++ b/solution.py
@@ -11,6 +11,10 @@
 BF16 = jnp.bfloat16
 LANES = 128
 SUB = 8
+
+
+def meetings_of(line_count):
+    return max(line_count // 2, 1).bit_length() - 1
 
 
 def build(dwell_shape, influence_shape, words, az_count, rad_count, tool_count):
@@ -21,6 +25,8 @@
     pairs = rows // 2
     field = rows * tiles
     steps = extent // 2 + 1
+    group = 11
+    assert steps % group == 0
     plane_count = 2 * rad_count * tool_count
     line_count = az_count // 2
     for count in (az_count, rad_count, tool_count):
@@ -76,9 +82,6 @@
         removal_edge,
         edge,
         gradient_new,
-        dwell_res,
-        residual_res,
-        direction_res,
         msg,
         box_a,
         box_b,
@@ -86,6 +89,7 @@
         halo_send,
         halo_recv,
         tool_sem,
+        meet,
         sum_send,
         sum_recv,
     ):
@@ -129,10 +133,10 @@
 
         for step in range(1, plane_count):
             greet(plane_peer(step))
-        for step in range(1, line_count):
-            greet(line_peer(step))
         outer = 1 - 2 * (1 - lax.rem(az, 2))
         greet(at(0, outer))
+        greet(at(0, 2))
+        greet(at(0, -2))
 
         @pl.when(has_up)
         def _():
@@ -163,7 +167,24 @@
             low_edge_out[side] = tile_of.astype(BF16)
 
         extra = 1 + has_up.astype(jnp.int32) + has_down.astype(jnp.int32)
-        pl.semaphore_wait(barrier, plane_count + line_count - 2 + extra)
+        pl.semaphore_wait(barrier, plane_count + 1 + extra)
+
+        meetings = meetings_of(line_count)
+
+        def meet_send(step):
+            if step < meetings:
+                for da in (2 << step, -(2 << step)):
+                    pl.semaphore_signal(meet.at[step], inc=1, device_id=at(0, da), device_id_type=MESH)
+
+        def meet_wait(step):
+            if step < meetings:
+                pl.semaphore_wait(meet.at[step], 2)
+
+        def meet_last():
+            for step in range(2, meetings):
+                if step > 2:
+                    meet_send(step)
+                meet_wait(step)
 
         def halo(phase, mid_src, mid_dst, edge_src, edge_dst):
             copies = []
@@ -190,12 +211,10 @@
                     else:
                         pl.when(has_down if d == 0 else has_up)(copy.start)
 
-            def wait_recv():
+            def wait_recv(block):
                 for d, copy in copies:
-                    if d == 1:
+                    if d == block:
                         copy.wait_recv()
-                    else:
-                        pl.when(has_up if d == 0 else has_down)(copy.wait_recv)
 
             def wait_send():
                 for d, copy in copies:
@@ -212,6 +231,7 @@
         removal_halo = halo(3, removal.at[1], removal, removal_edge_out, removal_edge)
 
         first_halo[0]()
+        meet_send(0)
 
         influence_copy.wait()
         j_of = lax.broadcasted_iota(jnp.int32, (extent, LANES), 0)
@@ -301,20 +321,20 @@
         def adjoint(out):
             acc[...] = jnp.zeros_like(acc)
 
-            @pl.loop(0, steps // 3)
+            @pl.loop(0, steps // group)
             def _(kk):
                 lhs = jnp.concatenate(
                     [
-                        win_adj[pl.ds(pl.multiple_of((3 * kk + u) * 16, 16), pairs * 16), :]
-                        for u in range(3)
+                        win_adj[pl.ds(pl.multiple_of((group * kk + u) * 16, 16), pairs * 16), :]
+                        for u in range(group)
                     ],
                     axis=1,
                 )
-                first = pl.multiple_of(6 * kk * LANES, LANES)
+                first = pl.multiple_of(2 * group * kk * LANES, LANES)
                 rhs = jnp.concatenate(
                     [
-                        band_adj[pl.ds(first + LANES, 6 * LANES), :],
-                        band_adj[pl.ds(first, 6 * LANES), :],
+                        band_adj[pl.ds(first + LANES, 2 * group * LANES), :],
+                        band_adj[pl.ds(first, 2 * group * LANES), :],
                     ],
                     axis=1,
                 )
@@ -362,19 +382,19 @@
             )
             return all_of
 
-        def total_of(first, side_work):
+        def total_of(first, beside_plane, beside_line):
             stage = sum_stage(first, first, box_a.at[first // 2], plane_count, plane_peer)
-            side_work()
+            beside_plane()
             stage.wait_recv()
             msg[first + 1] = msg[first] + jnp.sum(box_a[first // 2], axis=0)
             other = sum_stage(first + 1, first + 1, box_b.at[first // 2], line_count, line_peer)
+            beside_line()
             other.wait_recv()
             everything = msg[first + 1] + jnp.sum(box_b[first // 2], axis=0)
             return jnp.sum(everything, axis=1, keepdims=True), (stage, other)
 
-        first_halo[1]()
-
         def first_block(d):
+            first_halo[1](d)
             if d == 1:
                 edge[...] = low_edge_in[1].astype(F32)
                 assemble(win_adj, 1, lambda m: masked[1, at_pair(m), :])
@@ -389,6 +409,8 @@
         for side, tile in ((0, tiles - 1), (1, 0)):
             grad_edge_out[side] = gradient[pl.ds(tile, tools * rows, stride=tiles), :].astype(BF16)
         grad_halo[0]()
+        meet_wait(0)
+        meet_send(1)
 
         for t in range(tools):
 
@@ -397,9 +419,8 @@
                 at_q = pl.ds(pl.multiple_of(q * LANES, LANES), LANES)
                 band_fwd[t, at_q, :] = toeplitz(head_fwd[t, pl.ds(q, 1), :], extent + 1, 1)
 
-        grad_halo[1]()
-
         def grad_block(d):
+            grad_halo[1](d)
             for t in range(tools):
                 edge[...] = grad_edge_in[d, :, t * rows : (t + 1) * rows, :].astype(F32)
                 first = t * field
@@ -422,19 +443,19 @@
 
         acc_fwd[...] = jnp.zeros_like(acc_fwd)
 
-        @pl.loop(0, steps // 3)
+        @pl.loop(0, steps // group)
         def _(kk):
             lhs = jnp.concatenate(
                 [
-                    win_fwd[t, pl.ds(pl.multiple_of((3 * kk + u) * 16, 16), pairs * 16), :]
+                    win_fwd[t, pl.ds(pl.multiple_of((group * kk + u) * 16, 16), pairs * 16), :]
                     for t in range(tools)
-                    for u in range(3)
+                    for u in range(group)
                 ],
                 axis=1,
             )
-            first = pl.multiple_of(6 * kk * LANES, LANES)
+            first = pl.multiple_of(2 * group * kk * LANES, LANES)
             rhs = jnp.concatenate(
-                [band_fwd[t, pl.ds(first, 6 * LANES), :] for t in range(tools)], axis=0
+                [band_fwd[t, pl.ds(first, 2 * group * LANES), :] for t in range(tools)], axis=0
             )
             acc_fwd[...] += jnp.dot(lhs, rhs, preferred_element_type=F32)
 
@@ -461,6 +482,8 @@
             )
         for copy in tool_copies:
             copy.start()
+        meet_wait(1)
+        meet_send(2)
         for copy in tool_copies:
             copy.wait_recv()
 
@@ -473,8 +496,6 @@
             return total + value[:SUB] * value[:SUB] + value[SUB:] * value[SUB:]
 
         curvature_part = lax.fori_loop(0, pairs, join, jnp.zeros((SUB, LANES), F32), unroll=4)
-        for side, tile in ((0, tiles - 1), (1, 0)):
-            removal_edge_out[side] = removal[1, pl.ds(tile, rows, stride=tiles), :]
         msg[0] = jnp.concatenate(
             [
                 jnp.sum(gamma_part, axis=0, keepdims=True),
@@ -483,18 +504,20 @@
             axis=0,
         )
 
-        def beside():
-            removal_halo[0]()
-            masked_halo[1]()
-            removal_halo[1]()
+        def edges():
+            for side, tile in ((0, tiles - 1), (1, 0)):
+                removal_edge_out[side] = removal[1, pl.ds(tile, rows, stride=tiles), :]
             dwell_copy.wait()
-
-        sums, stages = total_of(0, beside)
+            meet_last()
+
+        sums, stages = total_of(0, edges, removal_halo[0])
         gamma = sums[0:1]
         curvature = sums[1:2] * (1.0 / tool_count)
         step_size = gamma / (curvature + EPSILON)
 
         def second_block(d):
+            masked_halo[1](d)
+            removal_halo[1](d)
             edge[...] = masked_edge[d] - step_size * removal_edge[d]
             assemble(
                 win_adj, d, lambda m: masked[d, at_pair(m), :] - step_size * removal[d, at_pair(m), :]
@@ -505,32 +528,27 @@
         new_row = jnp.sum(new_part, axis=0, keepdims=True)
         msg[2] = jnp.concatenate([new_row, new_row], axis=0)
 
-        dwell_store = pltpu.make_async_copy(dwell_res, dwell_out, local_sem.at[2])
-        residual_store = pltpu.make_async_copy(residual_res, residual_out, local_sem.at[3])
-        direction_store = pltpu.make_async_copy(direction_res, direction_out, local_sem.at[4])
-
-        def outputs():
+        def dwell_output():
             for t in range(tools):
                 for c in range(tiles):
                     cols = slice(c * LANES, (c + 1) * LANES)
                     step_of = gradient[pl.ds(t * field + c, rows, stride=tiles), :]
-                    dwell_res[t, :, cols] = dwell_v[t, :, cols] + step_size * step_of
-            dwell_store.start()
+                    dwell_out[t, :, cols] = dwell_v[t, :, cols] + step_size * step_of
+
+        def residual_output():
             for c in range(share_tiles):
                 from_c = pl.ds(tool * share_tiles + c, rows, stride=tiles)
-                residual_res[:, c * LANES : (c + 1) * LANES] = (
+                residual_out[:, c * LANES : (c + 1) * LANES] = (
                     whole[from_c, :] - step_size * removal[1, from_c, :]
                 )
-            residual_store.start()
-
-        new_sums, new_stages = total_of(2, outputs)
+
+        new_sums, new_stages = total_of(2, dwell_output, residual_output)
         ratio = new_sums[0:1] / (gamma + EPSILON)
         for t in range(tools):
             for c in range(tiles):
                 cols = slice(c * LANES, (c + 1) * LANES)
                 from_c = pl.ds(t * field + c, rows, stride=tiles)
-                direction_res[t, :, cols] = gradient_new[from_c, :] + ratio * gradient[from_c, :]
-        direction_store.start()
+                direction_out[t, :, cols] = gradient_new[from_c, :] + ratio * gradient[from_c, :]
 
         for phase in (first_halo, masked_halo, grad_halo, removal_halo):
             phase[2]()
@@ -538,9 +556,6 @@
             copy.wait_send()
         for stage in stages + new_stages:
             stage.wait_send()
-        dwell_store.wait()
-        residual_store.wait()
-        direction_store.wait()
 
     hbm_spec = pl.BlockSpec(memory_space=pltpu.HBM)
     scratch = [
@@ -578,9 +593,6 @@
         ((3, 2, rows, LANES), F32),
         ((2, rows, LANES), F32),
         ((tools * field, LANES), F32),
-        (dwell_shape, F32),
-        ((rows, share), F32),
-        (dwell_shape, F32),
         ((4, 2, LANES), F32),
         ((2, plane_count - 1, 2, LANES), F32),
         ((2, line_count - 1, 2, LANES), F32),
@@ -588,12 +600,12 @@
     return pl.pallas_call(
         body,
         out_shape=(
-            jax.ShapeDtypeStruct(dwell_shape, F32),
-            jax.ShapeDtypeStruct((rows, share), F32),
-            jax.ShapeDtypeStruct(dwell_shape, F32),
+            pltpu.VMEM(dwell_shape, F32),
+            pltpu.VMEM((rows, share), F32),
+            pltpu.VMEM(dwell_shape, F32),
         ),
         in_specs=[hbm_spec] * 6,
-        out_specs=(hbm_spec,) * 3,
+        out_specs=(pl.BlockSpec(memory_space=pltpu.VMEM),) * 3,
         scratch_shapes=[
             pltpu.VMEM(influence_shape, BF16),
             pltpu.SMEM((rows,), jnp.int32),
@@ -606,6 +618,7 @@
             pltpu.SemaphoreType.DMA((4, 9)),
             pltpu.SemaphoreType.DMA((4, 9)),
             pltpu.SemaphoreType.DMA((2, max(tool_count - 1, 1))),
+            pltpu.SemaphoreType.REGULAR((max(meetings_of(line_count), 1),)),
             pltpu.SemaphoreType.DMA((4,)),
             pltpu.SemaphoreType.DMA((4,)),
         ],

time: 73 us -> 64.7 us (0.89)
  Pallas kernels: 72.2 us -> 64 us
    pallas_call x1, Pallas kernels: 71.4 us -> 63.1 us  [per_device(): call(*(pltpu.with_memory_space_constraint(x, pltpu.HBM) for x in given))]
where the time goes in v3:
time: 64.7 us; the launch traced here: 64.6 us
  Pallas kernels  64 us (99%)
    pallas_call x1, Pallas kernels, per_device(): call(*(pltpu.with_memory_space_constraint(x, pltpu.HBM) for x in given))  63.1 us

profile of v3, /device:TPU:1, one launch (start us, length us, event | category | flops | bytes accessed | tf_op | source)
XLA Modules:
  0.0 64.6 jit_solution(3861095705222181509)
XLA Ops:
  0.6 63.1 %cgls.1 = (f32[2,32,1024]{2,1,0:T(8,128)S(1)}, f32[32,512]{1,0:T(8,128)S(1)}, f32[2,32,1024]{2,1,0:T(8,128)S(1)}) custom-call(f32[2,32,1024]{2,1,0:T(8,128)} %dwell_hbm.1, f32[32,1024]{1,0:T(8,128)} %residual_hbm.1, bf16[2,64,64]{2,1,0:T(8,128)(2,1)} %influence_hbm.1, s32[32]{0:T(128)} %start_hbm.1, s32[32]{0:T(128)} %end_hbm.1, s32[2,32,64]{2,1,0:T(8,128)} %bits_hbm.1), custom_call_target="tpu_custom_call" | custom-call | tf_op jit(solution)/shard_map/cgls/pallas_call | solution.py:666
  63.8 0.8 %hand_on.1 = (f32[2,32,1024]{2,1,0:T(8,128)}, f32[32,512]{1,0:T(8,128)}, f32[2,32,1024]{2,1,0:T(8,128)}) custom-call(f32[2,32,1024]{2,1,0:T(8,128)S(1)} %get-tuple-element.6.refs_0_, f32[32,512]{1,0:T(8,128)S(1)} %get-tuple-element.7.refs_1_, f32[2,32,1024]{2,1,0:T(8,128)S(1)} %get-tuple-element.8.refs_2_), custom_call_target="tpu_custom_call" | custom-call | tf_op jit(solution)/shard_map/hand_on/pallas_call | solution.py:645

commit v4 on v3

--- a/solution.py
+++ b/solution.py
@@ -82,6 +82,7 @@
         removal_edge,
         edge,
         gradient_new,
+        grad_natural,
         msg,
         box_a,
         box_b,
@@ -131,8 +132,6 @@
         def greet(peer):
             pl.semaphore_signal(barrier, inc=1, device_id=peer, device_id_type=MESH)
 
-        for step in range(1, plane_count):
-            greet(plane_peer(step))
         outer = 1 - 2 * (1 - lax.rem(az, 2))
         greet(at(0, outer))
         greet(at(0, 2))
@@ -145,6 +144,9 @@
         @pl.when(has_down)
         def _():
             greet(at(1, outer))
+
+        for step in range(1, plane_count):
+            greet(plane_peer(step))
 
         residual_copy.wait()
         for c in range(tiles):
@@ -187,48 +189,53 @@
                 meet_wait(step)
 
         def halo(phase, mid_src, mid_dst, edge_src, edge_dst):
-            copies = []
-            for d in (0, 2, 1):
-                for side, da in ((1, 0), (0, 1), (2, -1)):
-                    if d == 1 and side == 1:
-                        continue
-                    src = mid_src if side == 1 else edge_src.at[side // 2]
-                    dst = mid_dst.at[d] if side == 1 else edge_dst.at[d, side // 2]
-                    copy = pltpu.make_async_remote_copy(
-                        src_ref=src,
-                        dst_ref=dst,
-                        send_sem=halo_send.at[phase, 3 * d + side],
-                        recv_sem=halo_recv.at[phase, 3 * d + side],
-                        device_id=at(1 - d, da),
-                        device_id_type=MESH,
-                    )
-                    copies.append((d, copy))
+            sides = ((1, 0),) if mid_dst is not None else ()
+            sides += ((0, 1), (2, -1)) if edge_dst is not None else ()
+
+            def copy_of(d, side, da):
+                return pltpu.make_async_remote_copy(
+                    src_ref=mid_src if side == 1 else edge_src.at[side // 2],
+                    dst_ref=mid_dst(d) if side == 1 else edge_dst.at[d, side // 2],
+                    send_sem=halo_send.at[phase, 3 * d + side],
+                    recv_sem=halo_recv.at[phase, 3 * d + side],
+                    device_id=at(1 - d, da),
+                    device_id_type=MESH,
+                )
+
+            def of_block(d, act, own=False):
+                for side, da in sides:
+                    if not (own and side == 1):
+                        act(copy_of(d, side, da))
+
+            def to_all(act):
+                pl.when(has_down)(lambda: of_block(0, act))
+                pl.when(has_up)(lambda: of_block(2, act))
+                of_block(1, act, own=True)
 
             def start():
-                for d, copy in copies:
-                    if d == 1:
-                        copy.start()
-                    else:
-                        pl.when(has_down if d == 0 else has_up)(copy.start)
-
-            def wait_recv(block):
-                for d, copy in copies:
-                    if d == block:
-                        copy.wait_recv()
+                to_all(lambda copy: copy.start())
+
+            def wait_recv(d):
+                of_block(d, lambda copy: copy.wait_recv(), own=isinstance(d, int))
 
             def wait_send():
-                for d, copy in copies:
-                    if d == 1:
-                        copy.wait_send()
-                    else:
-                        pl.when(has_down if d == 0 else has_up)(copy.wait_send)
+                to_all(lambda copy: copy.wait_send())
 
             return start, wait_recv, wait_send
 
-        first_halo = halo(0, low_out, low_in, low_edge_out, low_edge_in)
-        masked_halo = halo(1, masked.at[1], masked, masked_edge_out, masked_edge)
-        grad_halo = halo(2, grad_low, grad_in, grad_edge_out, grad_edge_in)
-        removal_halo = halo(3, removal.at[1], removal, removal_edge_out, removal_edge)
+        first_halo = halo(0, low_out, lambda d: low_in.at[d], low_edge_out, low_edge_in)
+        masked_halo = halo(1, masked.at[1], lambda d: masked.at[d], masked_edge_out, masked_edge)
+        removal_halo = halo(3, removal.at[1], lambda d: removal.at[d], removal_edge_out, removal_edge)
+
+        def grad_phase(t):
+            mine = pl.ds(t * field, field)
+            edges_of = (grad_edge_out, grad_edge_in) if t == 0 else (None, None)
+            return halo(4 if t else 2, grad_low.at[mine], lambda d: grad_in.at[d, mine], *edges_of)
+
+        grad_halos = [grad_phase(t) for t in range(tools)]
+        near = 2 - 2 * lax.rem(rad, 2)
+        far = 2 - near
+        has_far = jnp.where(near == 2, rad, rad_count - 1 - rad) > 0
 
         first_halo[0]()
         meet_send(0)
@@ -289,7 +296,7 @@
             ).astype(F32)
 
         def assemble(target, d, two_rows):
-            @pl.loop(0, pairs, unroll=4)
+            @pl.loop(0, pairs, unroll=True)
             def _(m):
                 both = two_rows(m)
                 for a in range(2):
@@ -308,21 +315,25 @@
         def at_pair(m):
             return pl.ds(pl.multiple_of(m * 2 * tiles, 2 * tiles), 2 * tiles)
 
-        def fill_blank(target, d):
-            target[d * pairs * 16 : (d + 1) * pairs * 16, :] = jnp.zeros((pairs * 16, 2 * LANES), BF16)
-
-        def over_blocks(block, blank_of=None):
-            block(1)
-            for d, there in ((0, has_up), (2, has_down)):
-                pl.when(there)(lambda d=d: block(d))
-                if blank_of is not None:
-                    pl.when(jnp.logical_not(there))(lambda d=d: blank_of(d))
-
-        def adjoint(out):
+        def far_block(block, target=None):
+            pl.when(has_far)(lambda: block(far))
+            if target is not None:
+
+                @pl.when(jnp.logical_not(has_far))
+                def _():
+                    at_far = pl.ds(pl.multiple_of(far * pairs * 16, pairs * 16), pairs * 16)
+                    target[at_far, :] = jnp.zeros((pairs * 16, 2 * LANES), BF16)
+
+        def groups(step, far_ready):
+            @pl.loop(0, steps // group)
+            def _(i):
+                pl.when(i == 1)(far_ready)
+                step(near + i * (1 - near))
+
+        def adjoint(out, far_ready):
             acc[...] = jnp.zeros_like(acc)
 
-            @pl.loop(0, steps // group)
-            def _(kk):
+            def one(kk):
                 lhs = jnp.concatenate(
                     [
                         win_adj[pl.ds(pl.multiple_of((group * kk + u) * 16, 16), pairs * 16), :]
@@ -340,6 +351,8 @@
                 )
                 acc[...] += jnp.dot(lhs, rhs, preferred_element_type=F32)
 
+            groups(one, far_ready)
+
             def finish(m, total):
                 for b in range(2):
                     cols = slice(b * LANES, (b + 1) * LANES)
@@ -395,20 +408,24 @@
 
         def first_block(d):
             first_halo[1](d)
-            if d == 1:
-                edge[...] = low_edge_in[1].astype(F32)
-                assemble(win_adj, 1, lambda m: masked[1, at_pair(m), :])
+            edge[...] = low_edge_in[d].astype(F32)
+            if isinstance(d, int):
+                assemble(win_adj, d, lambda m: masked[d, at_pair(m), :])
             else:
-                edge[...] = low_edge_in[d].astype(F32)
                 assemble(win_adj, d, lambda m: low_in[d, at_pair(m), :].astype(F32))
 
-        over_blocks(first_block, lambda d: fill_blank(win_adj, d))
-        masked_halo[0]()
-        gamma_part = adjoint(gradient)
+        first_block(1)
+        first_block(near)
+
+        def first_far():
+            far_block(first_block, win_adj)
+
+        gamma_part = adjoint(gradient, first_far)
         grad_low[...] = gradient[...].astype(BF16)
         for side, tile in ((0, tiles - 1), (1, 0)):
             grad_edge_out[side] = gradient[pl.ds(tile, tools * rows, stride=tiles), :].astype(BF16)
-        grad_halo[0]()
+        for grad_halo in grad_halos:
+            grad_halo[0]()
         meet_wait(0)
         meet_send(1)
 
@@ -419,45 +436,38 @@
                 at_q = pl.ds(pl.multiple_of(q * LANES, LANES), LANES)
                 band_fwd[t, at_q, :] = toeplitz(head_fwd[t, pl.ds(q, 1), :], extent + 1, 1)
 
-        def grad_block(d):
-            grad_halo[1](d)
-            for t in range(tools):
+        acc_fwd[...] = jnp.zeros_like(acc_fwd)
+        for t in range(tools):
+
+            def grad_block(d, t=t):
+                grad_halos[t][1](d)
                 edge[...] = grad_edge_in[d, :, t * rows : (t + 1) * rows, :].astype(F32)
-                first = t * field
-                if d == 1:
-                    assemble(win_fwd.at[t], 1, lambda m, first=first: gradient[pl.ds(pl.multiple_of(first + m * 16, 16), 16), :])
+
+                def mine(m):
+                    return pl.ds(pl.multiple_of(t * field + m * 16, 16), 16)
+
+                if isinstance(d, int):
+                    assemble(win_fwd.at[t], d, lambda m: gradient[mine(m), :])
                 else:
-                    assemble(
-                        win_fwd.at[t],
-                        d,
-                        lambda m, first=first: grad_in[
-                            d, pl.ds(pl.multiple_of(first + m * 16, 16), 16), :
-                        ].astype(F32),
-                    )
-
-        def grad_blank(d):
-            for t in range(tools):
-                fill_blank(win_fwd.at[t], d)
-
-        over_blocks(grad_block, grad_blank)
-
-        acc_fwd[...] = jnp.zeros_like(acc_fwd)
-
-        @pl.loop(0, steps // group)
-        def _(kk):
-            lhs = jnp.concatenate(
-                [
-                    win_fwd[t, pl.ds(pl.multiple_of((group * kk + u) * 16, 16), pairs * 16), :]
-                    for t in range(tools)
-                    for u in range(group)
-                ],
-                axis=1,
-            )
-            first = pl.multiple_of(2 * group * kk * LANES, LANES)
-            rhs = jnp.concatenate(
-                [band_fwd[t, pl.ds(first, 2 * group * LANES), :] for t in range(tools)], axis=0
-            )
-            acc_fwd[...] += jnp.dot(lhs, rhs, preferred_element_type=F32)
+                    assemble(win_fwd.at[t], d, lambda m: grad_in[d, mine(m), :].astype(F32))
+
+            def one(kk, t=t):
+                lhs = jnp.concatenate(
+                    [
+                        win_fwd[t, pl.ds(pl.multiple_of((group * kk + u) * 16, 16), pairs * 16), :]
+                        for u in range(group)
+                    ],
+                    axis=1,
+                )
+                first = pl.multiple_of(2 * group * kk * LANES, LANES)
+                rhs = band_fwd[t, pl.ds(first, 2 * group * LANES), :]
+                acc_fwd[...] += jnp.dot(lhs, rhs, preferred_element_type=F32)
+
+            grad_block(1)
+            grad_block(near)
+            groups(one, lambda t=t, block=grad_block: far_block(block, win_fwd.at[t]))
+            if t == 0:
+                masked_halo[0]()
 
         @pl.loop(0, pairs, unroll=4)
         def _(m):
@@ -523,8 +533,9 @@
                 win_adj, d, lambda m: masked[d, at_pair(m), :] - step_size * removal[d, at_pair(m), :]
             )
 
-        over_blocks(second_block)
-        new_part = adjoint(gradient_new)
+        second_block(1)
+        second_block(near)
+        new_part = adjoint(gradient_new, lambda: far_block(second_block))
         new_row = jnp.sum(new_part, axis=0, keepdims=True)
         msg[2] = jnp.concatenate([new_row, new_row], axis=0)
 
@@ -533,9 +544,14 @@
                 for c in range(tiles):
                     cols = slice(c * LANES, (c + 1) * LANES)
                     step_of = gradient[pl.ds(t * field + c, rows, stride=tiles), :]
+                    grad_natural[t, :, cols] = step_of
                     dwell_out[t, :, cols] = dwell_v[t, :, cols] + step_size * step_of
 
         def residual_output():
+            for t in range(tools):
+                for c in range(tiles):
+                    from_c = pl.ds(t * field + c, rows, stride=tiles)
+                    direction_out[t, :, c * LANES : (c + 1) * LANES] = gradient_new[from_c, :]
             for c in range(share_tiles):
                 from_c = pl.ds(tool * share_tiles + c, rows, stride=tiles)
                 residual_out[:, c * LANES : (c + 1) * LANES] = (
@@ -545,12 +561,9 @@
         new_sums, new_stages = total_of(2, dwell_output, residual_output)
         ratio = new_sums[0:1] / (gamma + EPSILON)
         for t in range(tools):
-            for c in range(tiles):
-                cols = slice(c * LANES, (c + 1) * LANES)
-                from_c = pl.ds(t * field + c, rows, stride=tiles)
-                direction_out[t, :, cols] = gradient_new[from_c, :] + ratio * gradient[from_c, :]
-
-        for phase in (first_halo, masked_halo, grad_halo, removal_halo):
+            direction_out[t] = direction_out[t] + ratio * grad_natural[t]
+
+        for phase in (first_halo, masked_halo, *grad_halos, removal_halo):
             phase[2]()
         for copy in tool_copies:
             copy.wait_send()
@@ -593,6 +606,7 @@
         ((3, 2, rows, LANES), F32),
         ((2, rows, LANES), F32),
         ((tools * field, LANES), F32),
+        (dwell_shape, F32),
         ((4, 2, LANES), F32),
         ((2, plane_count - 1, 2, LANES), F32),
         ((2, line_count - 1, 2, LANES), F32),
@@ -615,8 +629,8 @@
         + [pltpu.VMEM(shape, dtype) for shape, dtype in scratch]
         + [
             pltpu.SemaphoreType.DMA((9,)),
-            pltpu.SemaphoreType.DMA((4, 9)),
-            pltpu.SemaphoreType.DMA((4, 9)),
+            pltpu.SemaphoreType.DMA((5, 9)),
+            pltpu.SemaphoreType.DMA((5, 9)),
             pltpu.SemaphoreType.DMA((2, max(tool_count - 1, 1))),
             pltpu.SemaphoreType.REGULAR((max(meetings_of(line_count), 1),)),
             pltpu.SemaphoreType.DMA((4,)),

time: 64.7 us -> 63.2 us (0.977)
  Pallas kernels: 64 us -> 62.4 us
    pallas_call x1, Pallas kernels: 63.1 us -> 61.6 us  [per_device(): call(*(pltpu.with_memory_space_constraint(x, pltpu.HBM) for x in given))]
where the time goes in v4:
time: 63.2 us; the launch traced here: 63 us
  Pallas kernels  62.4 us (99%)
  between operations  0.64 us (1%)
    pallas_call x1, Pallas kernels, per_device(): call(*(pltpu.with_memory_space_constraint(x, pltpu.HBM) for x in given))  61.6 us

profile of v4, /device:TPU:1, one launch (start us, length us, event | category | flops | bytes accessed | tf_op | source)
XLA Modules:
  0.0 63.0 jit_solution(11110467839621131142)
XLA Ops:
  0.6 61.6 %cgls.1 = (f32[2,32,1024]{2,1,0:T(8,128)S(1)}, f32[32,512]{1,0:T(8,128)S(1)}, f32[2,32,1024]{2,1,0:T(8,128)S(1)}) custom-call(f32[2,32,1024]{2,1,0:T(8,128)} %dwell_hbm.1, f32[32,1024]{1,0:T(8,128)} %residual_hbm.1, bf16[2,64,64]{2,1,0:T(8,128)(2,1)} %influence_hbm.1, s32[32]{0:T(128)} %start_hbm.1, s32[32]{0:T(128)} %end_hbm.1, s32[2,32,64]{2,1,0:T(8,128)} %bits_hbm.1), custom_call_target="tpu_custom_call" | custom-call | tf_op jit(solution)/shard_map/cgls/pallas_call | solution.py:680
  62.2 0.8 %hand_on.1 = (f32[2,32,1024]{2,1,0:T(8,128)}, f32[32,512]{1,0:T(8,128)}, f32[2,32,1024]{2,1,0:T(8,128)}) custom-call(f32[2,32,1024]{2,1,0:T(8,128)S(1)} %get-tuple-element.6.refs_0_, f32[32,512]{1,0:T(8,128)S(1)} %get-tuple-element.7.refs_1_, f32[2,32,1024]{2,1,0:T(8,128)S(1)} %get-tuple-element.8.refs_2_), custom_call_target="tpu_custom_call" | custom-call | tf_op jit(solution)/shard_map/hand_on/pallas_call | solution.py:659

commit v5 on v4

--- a/solution.py
+++ b/solution.py
@@ -26,7 +26,8 @@
     field = rows * tiles
     steps = extent // 2 + 1
     group = 11
-    assert steps % group == 0
+    quads, steps_fwd, group_fwd = rows // 4, extent // 2 + 2, 17
+    assert steps % group == 0 and steps_fwd % group_fwd == 0
     plane_count = 2 * rad_count * tool_count
     line_count = az_count // 2
     for count in (az_count, rad_count, tool_count):
@@ -267,7 +268,8 @@
         band_adj[LANES : 2 * LANES, :] = blank
         band_adj[(extent + 2) * LANES : (extent + 3) * LANES, :] = blank
         for t in range(tools):
-            band_fwd[t, (extent + 1) * LANES : (extent + 2) * LANES, :] = blank
+            band_fwd[t, 0 : 2 * LANES, :] = jnp.zeros((2 * LANES, LANES), BF16)
+            band_fwd[t, (extent + 3) * LANES :, :] = jnp.zeros((3 * LANES, LANES), BF16)
 
         def toeplitz(head, shift, which):
             square = jnp.broadcast_to(head, (LANES, LANES))
@@ -324,11 +326,11 @@
                     at_far = pl.ds(pl.multiple_of(far * pairs * 16, pairs * 16), pairs * 16)
                     target[at_far, :] = jnp.zeros((pairs * 16, 2 * LANES), BF16)
 
-        def groups(step, far_ready):
-            @pl.loop(0, steps // group)
+        def groups(count, step, far_ready):
+            @pl.loop(0, count)
             def _(i):
                 pl.when(i == 1)(far_ready)
-                step(near + i * (1 - near))
+                step(near // 2 * (count - 1) + i * (1 - near))
 
         def adjoint(out, far_ready):
             acc[...] = jnp.zeros_like(acc)
@@ -351,7 +353,7 @@
                 )
                 acc[...] += jnp.dot(lhs, rhs, preferred_element_type=F32)
 
-            groups(one, far_ready)
+            groups(steps // group, one, far_ready)
 
             def finish(m, total):
                 for b in range(2):
@@ -433,7 +435,7 @@
 
             @pl.loop(0, extent + 1, unroll=5)
             def _(q, t=t):
-                at_q = pl.ds(pl.multiple_of(q * LANES, LANES), LANES)
+                at_q = pl.ds(pl.multiple_of((q + 2) * LANES, LANES), LANES)
                 band_fwd[t, at_q, :] = toeplitz(head_fwd[t, pl.ds(q, 1), :], extent + 1, 1)
 
         acc_fwd[...] = jnp.zeros_like(acc_fwd)
@@ -452,31 +454,40 @@
                     assemble(win_fwd.at[t], d, lambda m: grad_in[d, mine(m), :].astype(F32))
 
             def one(kk, t=t):
-                lhs = jnp.concatenate(
-                    [
-                        win_fwd[t, pl.ds(pl.multiple_of((group * kk + u) * 16, 16), pairs * 16), :]
-                        for u in range(group)
-                    ],
+                def rows_of(u):
+                    return jnp.concatenate(
+                        [
+                            win_fwd[t, pl.ds(pl.multiple_of((group_fwd * kk + u + 2 * m) * 16, 16), 16), :]
+                            for m in range(quads)
+                        ],
+                        axis=0,
+                    )
+
+                lhs = jnp.concatenate([rows_of(u) for u in range(group_fwd)], axis=1)
+                first = pl.multiple_of(2 * group_fwd * kk * LANES, LANES)
+                span = 2 * group_fwd * LANES
+                rhs = jnp.concatenate(
+                    [band_fwd[t, pl.ds(first + 2 * LANES, span), :], band_fwd[t, pl.ds(first, span), :]],
                     axis=1,
                 )
-                first = pl.multiple_of(2 * group * kk * LANES, LANES)
-                rhs = band_fwd[t, pl.ds(first, 2 * group * LANES), :]
                 acc_fwd[...] += jnp.dot(lhs, rhs, preferred_element_type=F32)
 
             grad_block(1)
             grad_block(near)
-            groups(one, lambda t=t, block=grad_block: far_block(block, win_fwd.at[t]))
+            groups(steps_fwd // group_fwd, one, lambda t=t, block=grad_block: far_block(block, win_fwd.at[t]))
             if t == 0:
                 masked_halo[0]()
 
-        @pl.loop(0, pairs, unroll=4)
+        @pl.loop(0, quads, unroll=4)
         def _(m):
-            even = acc_fwd[pl.ds(pl.multiple_of(m * 16, 16), 8), :]
-            odd = acc_fwd[pl.ds(pl.multiple_of(m * 16 + 8, 8), 8), :]
-            top = jnp.where(left_half, even, pltpu.roll(odd, 64, axis=1))
-            low = jnp.where(left_half, pltpu.roll(even, 64, axis=1), odd)
-            at_m = at_pair(m)
-            part[at_m, :] = inside[at_m, :] * jnp.concatenate([top, low], axis=0)
+            for h in range(2):
+                cols = slice(h * LANES, (h + 1) * LANES)
+                even = acc_fwd[pl.ds(pl.multiple_of(m * 16, 16), 8), cols]
+                odd = acc_fwd[pl.ds(pl.multiple_of(m * 16 + 8, 8), 8), cols]
+                top = jnp.where(left_half, even, pltpu.roll(odd, 64, axis=1))
+                low = jnp.where(left_half, pltpu.roll(even, 64, axis=1), odd)
+                at_m = at_pair(2 * m + h)
+                part[at_m, :] = inside[at_m, :] * jnp.concatenate([top, low], axis=0)
 
         tool_copies = []
         for step in range(1, tool_count):
@@ -589,11 +600,11 @@
         ((tools, extent + 8, LANES), F32),
         ((2, LANES, LANES), F32),
         (((extent + 3) * LANES, LANES), BF16),
-        ((tools, (extent + 2) * LANES, LANES), BF16),
+        ((tools, (extent + 6) * LANES, LANES), BF16),
         ((3 * pairs * 16, 2 * LANES), BF16),
         ((tools, 3 * pairs * 16, 2 * LANES), BF16),
         ((pairs * 16, 2 * LANES), F32),
-        ((pairs * 16, LANES), F32),
+        ((quads * 16, 2 * LANES), F32),
         ((tools * field, LANES), F32),
         ((tools * field, LANES), BF16),
         ((2, tools * rows, LANES), BF16),

time: 63.2 us -> 62 us (0.981)
  Pallas kernels: 62.4 us -> 61.2 us
    pallas_call x1, Pallas kernels: 61.6 us -> 60.3 us  [per_device(): call(*(pltpu.with_memory_space_constraint(x, pltpu.HBM) for x in given))]
where the time goes in v5:
time: 62 us; the launch traced here: 61.8 us
  Pallas kernels  61.2 us (99%)
  between operations  0.64 us (1%)
    pallas_call x1, Pallas kernels, per_device(): call(*(pltpu.with_memory_space_constraint(x, pltpu.HBM) for x in given))  60.3 us

profile of v5, /device:TPU:1, one launch (start us, length us, event | category | flops | bytes accessed | tf_op | source)
XLA Modules:
  0.0 61.8 jit_solution(17909671236627253670)
XLA Ops:
  0.6 60.3 %cgls.1 = (f32[2,32,1024]{2,1,0:T(8,128)S(1)}, f32[32,512]{1,0:T(8,128)S(1)}, f32[2,32,1024]{2,1,0:T(8,128)S(1)}) custom-call(f32[2,32,1024]{2,1,0:T(8,128)} %dwell_hbm.1, f32[32,1024]{1,0:T(8,128)} %residual_hbm.1, bf16[2,64,64]{2,1,0:T(8,128)(2,1)} %influence_hbm.1, s32[32]{0:T(128)} %start_hbm.1, s32[32]{0:T(128)} %end_hbm.1, s32[2,32,64]{2,1,0:T(8,128)} %bits_hbm.1), custom_call_target="tpu_custom_call" | custom-call | tf_op jit(solution)/shard_map/cgls/pallas_call | solution.py:691
  61.0 0.8 %hand_on.1 = (f32[2,32,1024]{2,1,0:T(8,128)}, f32[32,512]{1,0:T(8,128)}, f32[2,32,1024]{2,1,0:T(8,128)}) custom-call(f32[2,32,1024]{2,1,0:T(8,128)S(1)} %get-tuple-element.6.refs_0_, f32[32,512]{1,0:T(8,128)S(1)} %get-tuple-element.7.refs_1_, f32[2,32,1024]{2,1,0:T(8,128)S(1)} %get-tuple-element.8.refs_2_), custom_call_target="tpu_custom_call" | custom-call | tf_op jit(solution)/shard_map/hand_on/pallas_call | solution.py:670

commit v6 on v5

--- a/solution.py
+++ b/solution.py
@@ -92,6 +92,7 @@
         halo_recv,
         tool_sem,
         meet,
+        plane_meet,
         sum_send,
         sum_recv,
     ):
@@ -133,21 +134,16 @@
         def greet(peer):
             pl.semaphore_signal(barrier, inc=1, device_id=peer, device_id_type=MESH)
 
-        outer = 1 - 2 * (1 - lax.rem(az, 2))
-        greet(at(0, outer))
-        greet(at(0, 2))
-        greet(at(0, -2))
-
-        @pl.when(has_up)
-        def _():
-            greet(at(-1, outer))
-
-        @pl.when(has_down)
-        def _():
-            greet(at(1, outer))
-
-        for step in range(1, plane_count):
-            greet(plane_peer(step))
+        for da in (1, -1, 2, -2):
+            greet(at(0, da))
+        for step in range(1, tool_count):
+            greet({"az": az, "rad": rad, "tool": tool ^ step})
+        for there, dr in ((has_up, -1), (has_down, 1)):
+
+            @pl.when(there)
+            def _(dr=dr):
+                for da in (0, 1, -1):
+                    greet(at(dr, da))
 
         residual_copy.wait()
         for c in range(tiles):
@@ -169,8 +165,34 @@
             masked_edge_out[side] = tile_of
             low_edge_out[side] = tile_of.astype(BF16)
 
-        extra = 1 + has_up.astype(jnp.int32) + has_down.astype(jnp.int32)
-        pl.semaphore_wait(barrier, plane_count + 1 + extra)
+        beside = has_up.astype(jnp.int32) + has_down.astype(jnp.int32)
+        pl.semaphore_wait(barrier, 3 + tool_count + 3 * beside)
+
+        rad_meetings = (rad_count - 1).bit_length()
+
+        def tell(which, peer):
+            pl.semaphore_signal(plane_meet.at[which], inc=1, device_id=peer, device_id_type=MESH)
+
+        def rad_send(step):
+            if step < rad_meetings:
+                reach = 1 << step
+                pl.when(rad >= reach)(lambda: tell(step, at(-reach, 0)))
+                pl.when(rad + reach < rad_count)(lambda: tell(step, at(reach, 0)))
+
+        def rad_wait(step):
+            if step < rad_meetings:
+                reach = 1 << step
+                known = (rad >= reach).astype(jnp.int32) + (rad + reach < rad_count).astype(jnp.int32)
+                pl.semaphore_wait(plane_meet.at[step], known)
+
+        def cross_send(step):
+            if step == 0:
+                for other in range(1, tool_count):
+                    tell(rad_meetings, {"az": az, "rad": rad, "tool": tool ^ other})
+            tell(rad_meetings + step, {"az": az ^ 1, "rad": rad, "tool": tool})
+
+        def cross_wait(step):
+            pl.semaphore_wait(plane_meet.at[rad_meetings + step], 1 if step else tool_count)
 
         meetings = meetings_of(line_count)
 
@@ -240,6 +262,7 @@
 
         first_halo[0]()
         meet_send(0)
+        rad_send(0)
 
         influence_copy.wait()
         j_of = lax.broadcasted_iota(jnp.int32, (extent, LANES), 0)
@@ -418,6 +441,8 @@
 
         first_block(1)
         first_block(near)
+        rad_wait(0)
+        rad_send(1)
 
         def first_far():
             far_block(first_block, win_adj)
@@ -430,6 +455,8 @@
             grad_halo[0]()
         meet_wait(0)
         meet_send(1)
+        rad_wait(1)
+        rad_send(2)
 
         for t in range(tools):
 
@@ -477,6 +504,11 @@
             groups(steps_fwd // group_fwd, one, lambda t=t, block=grad_block: far_block(block, win_fwd.at[t]))
             if t == 0:
                 masked_halo[0]()
+                for step in range(2, rad_meetings):
+                    if step > 2:
+                        rad_send(step)
+                    rad_wait(step)
+                cross_send(0)
 
         @pl.loop(0, quads, unroll=4)
         def _(m):
@@ -505,6 +537,8 @@
             copy.start()
         meet_wait(1)
         meet_send(2)
+        cross_wait(0)
+        cross_send(1)
         for copy in tool_copies:
             copy.wait_recv()
 
@@ -531,6 +565,7 @@
             dwell_copy.wait()
             meet_last()
 
+        cross_wait(1)
         sums, stages = total_of(0, edges, removal_halo[0])
         gamma = sums[0:1]
         curvature = sums[1:2] * (1.0 / tool_count)
@@ -644,6 +679,7 @@
             pltpu.SemaphoreType.DMA((5, 9)),
             pltpu.SemaphoreType.DMA((2, max(tool_count - 1, 1))),
             pltpu.SemaphoreType.REGULAR((max(meetings_of(line_count), 1),)),
+            pltpu.SemaphoreType.REGULAR(((rad_count - 1).bit_length() + 2,)),
             pltpu.SemaphoreType.DMA((4,)),
             pltpu.SemaphoreType.DMA((4,)),
         ],

time: 62 us -> 61.3 us (0.989)
  Pallas kernels: 61.2 us -> 60.5 us
    pallas_call x1, Pallas kernels: 60.3 us -> 59.7 us  [per_device(): call(*(pltpu.with_memory_space_constraint(x, pltpu.HBM) for x in given))]
where the time goes in v6:
time: 61.3 us; the launch traced here: 61.1 us
  Pallas kernels  60.5 us (99%)
  between operations  0.64 us (1%)
    pallas_call x1, Pallas kernels, per_device(): call(*(pltpu.with_memory_space_constraint(x, pltpu.HBM) for x in given))  59.7 us

profile of v6, /device:TPU:1, one launch (start us, length us, event | category | flops | bytes accessed | tf_op | source)
XLA Modules:
  0.0 61.1 jit_solution(5097479487319544214)
XLA Ops:
  0.6 59.7 %cgls.1 = (f32[2,32,1024]{2,1,0:T(8,128)S(1)}, f32[32,512]{1,0:T(8,128)S(1)}, f32[2,32,1024]{2,1,0:T(8,128)S(1)}) custom-call(f32[2,32,1024]{2,1,0:T(8,128)} %dwell_hbm.1, f32[32,1024]{1,0:T(8,128)} %residual_hbm.1, bf16[2,64,64]{2,1,0:T(8,128)(2,1)} %influence_hbm.1, s32[32]{0:T(128)} %start_hbm.1, s32[32]{0:T(128)} %end_hbm.1, s32[2,32,64]{2,1,0:T(8,128)} %bits_hbm.1), custom_call_target="tpu_custom_call" | custom-call | tf_op jit(solution)/shard_map/cgls/pallas_call | solution.py:727
  60.3 0.8 %hand_on.1 = (f32[2,32,1024]{2,1,0:T(8,128)}, f32[32,512]{1,0:T(8,128)}, f32[2,32,1024]{2,1,0:T(8,128)}) custom-call(f32[2,32,1024]{2,1,0:T(8,128)S(1)} %get-tuple-element.6.refs_0_, f32[32,512]{1,0:T(8,128)S(1)} %get-tuple-element.7.refs_1_, f32[2,32,1024]{2,1,0:T(8,128)S(1)} %get-tuple-element.8.refs_2_), custom_call_target="tpu_custom_call" | custom-call | tf_op jit(solution)/shard_map/hand_on/pallas_call | solution.py:706

commit v7 on v6

--- a/solution.py
+++ b/solution.py
@@ -107,8 +107,6 @@
         influence_copy = pltpu.make_async_copy(influence_hbm, influence_ref, local_sem.at[7])
         bits_copy = pltpu.make_async_copy(bits_hbm, bits_ref, local_sem.at[8])
         dwell_copy = pltpu.make_async_copy(dwell_hbm, dwell_v, local_sem.at[1])
-        for copy in (residual_copy, start_copy, end_copy, influence_copy, bits_copy, dwell_copy):
-            copy.start()
 
         def at(dr, da):
             return {
@@ -144,6 +142,9 @@
             def _(dr=dr):
                 for da in (0, 1, -1):
                     greet(at(dr, da))
+
+        for copy in (residual_copy, start_copy, end_copy, influence_copy, bits_copy, dwell_copy):
+            copy.start()
 
         residual_copy.wait()
         for c in range(tiles):
@@ -356,8 +357,6 @@
                 step(near // 2 * (count - 1) + i * (1 - near))
 
         def adjoint(out, far_ready):
-            acc[...] = jnp.zeros_like(acc)
-
             def one(kk):
                 lhs = jnp.concatenate(
                     [
@@ -439,6 +438,7 @@
             else:
                 assemble(win_adj, d, lambda m: low_in[d, at_pair(m), :].astype(F32))
 
+        acc[...] = jnp.zeros_like(acc)
         first_block(1)
         first_block(near)
         rad_wait(0)
@@ -448,11 +448,12 @@
             far_block(first_block, win_adj)
 
         gamma_part = adjoint(gradient, first_far)
-        grad_low[...] = gradient[...].astype(BF16)
         for side, tile in ((0, tiles - 1), (1, 0)):
             grad_edge_out[side] = gradient[pl.ds(tile, tools * rows, stride=tiles), :].astype(BF16)
-        for grad_halo in grad_halos:
-            grad_halo[0]()
+        for t in range(tools):
+            mine = slice(t * field, (t + 1) * field)
+            grad_low[mine, :] = gradient[mine, :].astype(BF16)
+            grad_halos[t][0]()
         meet_wait(0)
         meet_send(1)
         rad_wait(1)
@@ -564,6 +565,7 @@
                 removal_edge_out[side] = removal[1, pl.ds(tile, rows, stride=tiles), :]
             dwell_copy.wait()
             meet_last()
+            acc[...] = jnp.zeros_like(acc)
 
         cross_wait(1)
         sums, stages = total_of(0, edges, removal_halo[0])

time: 61.3 us -> 61.2 us (level)
  no operation moved by 1% of the time
where the time goes in v7:
time: 61.2 us; the launch traced here: 61.1 us
  Pallas kernels  60.5 us (99%)
  between operations  0.64 us (1%)
    pallas_call x1, Pallas kernels, per_device(): call(*(pltpu.with_memory_space_constraint(x, pltpu.HBM) for x in given))  59.6 us

profile of v7, /device:TPU:1, one launch (start us, length us, event | category | flops | bytes accessed | tf_op | source)
XLA Modules:
  0.0 61.1 jit_solution(24056851169400799)
XLA Ops:
  0.6 59.6 %cgls.1 = (f32[2,32,1024]{2,1,0:T(8,128)S(1)}, f32[32,512]{1,0:T(8,128)S(1)}, f32[2,32,1024]{2,1,0:T(8,128)S(1)}) custom-call(f32[2,32,1024]{2,1,0:T(8,128)} %dwell_hbm.1, f32[32,1024]{1,0:T(8,128)} %residual_hbm.1, bf16[2,64,64]{2,1,0:T(8,128)(2,1)} %influence_hbm.1, s32[32]{0:T(128)} %start_hbm.1, s32[32]{0:T(128)} %end_hbm.1, s32[2,32,64]{2,1,0:T(8,128)} %bits_hbm.1), custom_call_target="tpu_custom_call" | custom-call | tf_op jit(solution)/shard_map/cgls/pallas_call | solution.py:729
  60.3 0.8 %hand_on.1 = (f32[2,32,1024]{2,1,0:T(8,128)}, f32[32,512]{1,0:T(8,128)}, f32[2,32,1024]{2,1,0:T(8,128)}) custom-call(f32[2,32,1024]{2,1,0:T(8,128)S(1)} %get-tuple-element.6.refs_0_, f32[32,512]{1,0:T(8,128)S(1)} %get-tuple-element.7.refs_1_, f32[2,32,1024]{2,1,0:T(8,128)S(1)} %get-tuple-element.8.refs_2_), custom_call_target="tpu_custom_call" | custom-call | tf_op jit(solution)/shard_map/hand_on/pallas_call | solution.py:708
